TPU v7x, 256 devices: a whole 4x4x8 slice. The times are simulated.
256 devices in a mesh: branch: 4 (over x_hi, core), ty: 8 (over x_lo, y), tx: 8 (over z).
Axes of the slice: x: 4 (x_hi: 2, x_lo: 2; x = x_hi * 2 + x_lo), y: 4, z: 8, core: 2. Of those that a mesh axis runs over, the one named last changes fastest.
Arguments:
- feat0: bfloat16 [48, 512, 512], P(None, 'ty', 'tx'), may hold values from -6 to 6
- feat1: bfloat16 [96, 256, 256], P(None, 'ty', 'tx'), may hold values from -6 to 6
- feat2: bfloat16 [192, 128, 128], P(None, 'ty', 'tx'), may hold values from -6 to 6
- feat3: bfloat16 [384, 64, 64], P(None, 'ty', 'tx'), may hold values from -6 to 6
- block_w0: bfloat16 [2, 48, 432], replicated, may hold values from -0.3125 to 0.3125
- block_w1: bfloat16 [2, 96, 864], replicated, may hold values from -0.21875 to 0.21875
- block_w2: bfloat16 [2, 192, 1728], replicated, may hold values from -0.15625 to 0.15625
- block_w3: bfloat16 [2, 384, 3456], replicated, may hold values from -0.109375 to 0.109375
- block_b0: float32 [2, 48], replicated, may hold values from -1.8 to 1.8
- block_b1: float32 [2, 96], replicated, may hold values from -1.8 to 1.8
- block_b2: float32 [2, 192], replicated, may hold values from -1.8 to 1.8
- block_b3: float32 [2, 384], replicated, may hold values from -1.8 to 1.8
- up_w1: bfloat16 [1, 48, 96], replicated, may hold values from -0.625 to 0.625
- up_w2: bfloat16 [1, 144, 192], replicated, may hold values from -0.4375 to 0.4375
- up_w3: bfloat16 [1, 336, 384], replicated, may hold values from -0.3125 to 0.3125
- down_mid0: bfloat16 [1, 3, 48, 432], replicated, may hold values from -0.3125 to 0.3125
- down_mid1: bfloat16 [1, 1, 96, 864], replicated, may hold values from -0.21875 to 0.21875
- down_fin0: bfloat16 [1, 672, 432], replicated, may hold values from -0.3125 to 0.3125
- down_fin1: bfloat16 [1, 576, 864], replicated, may hold values from -0.21875 to 0.21875
- down_fin2: bfloat16 [1, 384, 1728], replicated, may hold values from -0.15625 to 0.15625
Outputs:
- joined0: bfloat16 [48, 512, 512], P(None, 'ty', 'tx')
- joined1: bfloat16 [96, 256, 256], P(None, 'ty', 'tx')
- joined2: bfloat16 [192, 128, 128], P(None, 'ty', 'tx')
- joined3: bfloat16 [384, 64, 64], P(None, 'ty', 'tx')
All inputs are finite; a program needn't handle non-finite values.
Results may differ from a plain program's by a relative error of at most 0.0095.
Values may be sent and summed in bfloat16 or wider, within the bound.
No kernel may reach another device: no remote copies, remote signals or barrier semaphores. Data moves between devices by JAX's collectives and lax.ppermute only.
A program may use at most 128 MiB of HBM per device.

v0:
```python
import functools

import jax
import jax.numpy as jnp
from jax import lax
from jax.experimental import pallas as pl
from jax.experimental.pallas import tpu as pltpu
from jax.sharding import PartitionSpec as P

BF = jnp.bfloat16
F32 = jnp.float32
TILE = (64, 32, 16, 8)
CHAN = (48, 96, 192, 384)
LEAD = (9, 5, 3, 2)
EXT = (75, 39, 21, 12)
PITCH = (80, 48, 32, 16)
TALL = (80, 48, 32, 16)
GROUP = (16, 16, 16, 8)
DOWN_ROWS, UP_ROWS = 592, 240
RIGHT_ROWS, LEFT_ROWS = 928, 400
PARAMS = pltpu.CompilerParams(vmem_limit_bytes=56 * 2**20)


def spans(chan):
    return [(lo, min(lo + 128, chan)) for lo in range(0, chan, 128)]


def put_packed(ref, at, value, branch, split):
    if branch == 0:
        ref[at : at + split, 0:48] = value[:split]
        ref[at : at + value.shape[0] - split, 64:112] = value[split:]
        return at + split
    for lo, hi in spans(CHAN[branch]):
        ref[at : at + value.shape[0], 0 : hi - lo] = value[:, lo:hi]
        at += value.shape[0]
    return at


def take_packed(ref, at, count, branch, split):
    if branch == 0:
        return jnp.concatenate(
            [ref[at : at + split, 0:48], ref[at : at + count - split, 64:112]], axis=0
        ), at + split
    parts = []
    for lo, hi in spans(CHAN[branch]):
        parts.append(ref[at : at + count, 0 : hi - lo])
        at += count
    return (parts[0] if len(parts) == 1 else jnp.concatenate(parts, axis=1)), at


def flat_rows(ref, lo, hi, branch):
    side = TILE[branch]
    value = ref[lo:hi].astype(F32)
    return value.reshape((hi - lo) * side, CHAN[branch]).astype(BF)


def pack_rows(f0, f1, f2, f3, down, up):
    at = 0
    for b, f in enumerate((f0, f1, f2, f3)):
        at = put_packed(down, at, flat_rows(f, TILE[b] - LEAD[b], TILE[b], b), b, 288)
    at = 0
    for b, f in enumerate((f0, f1, f2, f3)):
        at = put_packed(up, at, flat_rows(f, 0, 2, b), b, 64)


def pack_cols(f0, f1, f2, f3, above, below, right, left, work):
    down_at = up_at = right_at = left_at = 0
    for b, f in enumerate((f0, f1, f2, f3)):
        side, lead, chan, group = TILE[b], LEAD[b], CHAN[b], GROUP[b]
        high, down_at = take_packed(above, down_at, lead * side, b, 288)
        low, up_at = take_packed(below, up_at, 2 * side, b, 64)
        parts = (
            (high.astype(F32).reshape(lead, side, chan), 0, lead),
            (f[...].astype(F32).reshape(side, side, chan), lead, side),
            (low.astype(F32).reshape(2, side, chan), lead + side, 2),
        )
        for last in (True, False):
            cut = slice(side - group, side) if last else slice(0, group)
            for value, start, count in parts:
                edge = value[:, cut].reshape(count * group, chan)
                for s, (lo, hi) in enumerate(spans(chan)):
                    work[s, start * group : (start + count) * group, 0 : hi - lo] = edge[:, lo:hi]
            columns = range(group - lead, group) if last else range(2)
            cols = []
            for k in columns:
                planes = [
                    work[s, pl.ds(k, TALL[b], stride=group), 0 : hi - lo]
                    for s, (lo, hi) in enumerate(spans(chan))
                ]
                cols.append([p.astype(BF) for p in planes])
            target, at = (right, right_at) if last else (left, left_at)
            if b == 0:
                half = 5 if last else 1
                for i, (col,) in enumerate(cols):
                    place = at + (i if i < half else i - half) * TALL[0]
                    lane = 0 if i < half else 64
                    target[place : place + TALL[0], lane : lane + 48] = col
                at += half * TALL[0]
            else:
                for s, (lo, hi) in enumerate(spans(chan)):
                    for col in cols:
                        target[at : at + TALL[b], 0 : hi - lo] = col[s]
                        at += TALL[b]
            if last:
                right_at = at
            else:
                left_at = at


def clear_edges(place, planes, pitch, height, breadth, lead, trail):
    ty, tx = place[0], place[1]

    def rows(lo, count):
        for ref in planes:
            ref[lo * pitch : (lo + count) * pitch] = jnp.zeros((count * pitch, ref.shape[1]), F32)

    def cols(lo, count):
        for ref in planes:
            for k in range(lo, lo + count):
                ref[pl.ds(k, height, stride=pitch), :] = jnp.zeros((height, ref.shape[1]), F32)

    if lead:
        pl.when(ty == 0)(lambda: rows(0, lead))
        pl.when(tx == 0)(lambda: cols(0, lead))
    if trail:
        pl.when(ty == 7)(lambda: rows(height - trail, trail))
        pl.when(tx == 7)(lambda: cols(breadth - trail, trail))


def dot_nt(x, w):
    return lax.dot_general(x, w, (((1,), (1,)), ((), ())), preferred_element_type=F32)


def rounded(x):
    return x.astype(BF).astype(F32)


def main(
    place, f0, f1, f2, f3, above, below, cl, cr,
    w0, w1, w2, w3, b0, b1, b2, b3, u1, u2, u3, d01, d02, d12, fin03, fin13, fin23,
    j0, j1, j2, j3,
    x0, h0, a0, s0, t0, v01, v0, t02w, vv02, n03,
    x1, h1, a1, s1, t1, vv12, m13,
    x2, h2, a2, s2,
    x3, h3, a3, s3,
    z1, z2, y2, y1, wide, mcol,
):
    feats = (f0, f1, f2, f3)
    xs = ([x0], [x1], [x2.at[0], x2.at[1]], [x3.at[i] for i in range(3)])
    hs = ([h0], [h1], [h2.at[0], h2.at[1]], [h3.at[i] for i in range(3)])
    as_ = ([a0], [a1], [a2.at[0], a2.at[1]], [a3.at[i] for i in range(3)])
    x1[:, 96:128] = jnp.zeros((x1.shape[0], 32), F32)
    h1[:, 96:128] = jnp.zeros((h1.shape[0], 32), F32)
    a1[:, 96:128] = jnp.zeros((a1.shape[0], 32), F32)
    s0[...] = jnp.zeros_like(s0)
    t0[...] = jnp.zeros_like(t0)
    s2[...] = jnp.zeros_like(s2)

    def assemble(b, ats):
        side, lead, chan, pitch = TILE[b], LEAD[b], CHAN[b], PITCH[b]
        down_at, up_at, right_at, left_at = ats
        high, down_at = take_packed(above, down_at, lead * side, b, 288)
        low, up_at = take_packed(below, up_at, 2 * side, b, 64)
        for value, start, count in ((high, 0, lead), (low, lead + side, 2)):
            for y in range(count):
                row = value[y * side : (y + 1) * side].astype(F32)
                for s, (lo, hi) in enumerate(spans(chan)):
                    xs[b][s][pl.ds((start + y) * pitch + lead, side), 0 : hi - lo] = row[:, lo:hi]

        for y in range(side):
            row = feats[b][y].astype(F32)
            for s, (lo, hi) in enumerate(spans(chan)):
                xs[b][s][pl.ds((lead + y) * pitch + lead, side), 0 : hi - lo] = row[:, lo:hi]
        for ref, at, count, first, half in ((cl, right_at, lead, 0, 5), (cr, left_at, 2, lead + side, 1)):
            if b == 0:
                for i in range(count):
                    spot = at + (i if i < half else i - half) * TALL[0]
                    lane = 0 if i < half else 64
                    col = ref[spot : spot + TALL[0], lane : lane + 48].astype(F32)
                    x0[pl.ds(first + i, EXT[0], stride=pitch), 0:48] = col[: EXT[0]]
                at += half * TALL[0]
            else:
                for s, (lo, hi) in enumerate(spans(chan)):
                    for i in range(count):
                        col = ref[at : at + TALL[b], 0 : hi - lo].astype(F32)
                        xs[b][s][pl.ds(first + i, EXT[b], stride=pitch), 0 : hi - lo] = col[: EXT[b]]
                        at += TALL[b]
            if ref is cl:
                right_at = at
            else:
                left_at = at
        clear_edges(place, xs[b], pitch, EXT[b], EXT[b], lead, 2)
        return down_at, up_at, right_at, left_at

    ats = (0, 0, 0, 0)
    for b in range(4):
        ats = assemble(b, ats)

    def spread(planes, target, rows, step, slot, chan, lanes):
        @pl.loop(0, rows // step)
        def _(i):
            p = pl.multiple_of(i * step, step)
            for dx in range(3):
                for s, (lo, hi) in enumerate(spans(lanes)):
                    piece = planes[s][pl.ds(p + dx, step), 0 : hi - lo].astype(BF)
                    target[pl.ds(p, step), dx * slot + lo : dx * slot + hi] = piece

    def conv_loop(source, weight, rows, step, pitch, width, finish):
        @pl.loop(0, rows // step)
        def _(i):
            p = pl.multiple_of(i * step, step)
            total = None
            for dy in range(3):
                part = dot_nt(source[pl.ds(p + dy * pitch, step), 0:width], weight(dy))
                total = part if total is None else total + part
            finish(p, total)

    def block(b, weight, bias, source, slot, lanes, width, inner_rows, outer_rows, step, copy_step):
        pitch, chan, lead = PITCH[b], CHAN[b], LEAD[b]

        def inner(p, total):
            value = jnp.maximum(total + bias[0:1, :], 0.0)
            for s, (lo, hi) in enumerate(spans(chan)):
                hs[b][s][pl.ds(p, step), 0 : hi - lo] = value[:, lo:hi]

        def outer(p, total):
            total = total + bias[1:2, :]
            for s, (lo, hi) in enumerate(spans(chan)):
                kept = xs[b][s][pl.ds(p + 2 * pitch + 2, step), 0 : hi - lo]
                value = rounded(jnp.maximum(kept + total[:, lo:hi], 0.0))
                as_[b][s][pl.ds(p, step), 0 : hi - lo] = value

        spread(xs[b], source, inner_rows + 2 * pitch, copy_step, slot, chan, lanes)
        conv_loop(source, lambda dy: weight(0, dy), inner_rows, step, pitch, width, inner)
        clear_edges(place, hs[b], pitch, EXT[b] - 2, EXT[b] - 2, lead - 1, 1)
        spread(hs[b], source, outer_rows + 2 * pitch, copy_step, slot, chan, lanes)
        conv_loop(source, lambda dy: weight(1, dy), outer_rows, step, pitch, width, outer)
        clear_edges(place, as_[b], pitch, EXT[b] - 4, EXT[b] - 4, lead - 2, 0)

    block(0, lambda i, dy: w0[i, dy], b0, s0, 64, 48, 192, 76 * 80, 72 * 80, 320, 160)
    block(1, lambda i, dy: w1[i, dy], b1, s1, 128, 128, 384, 40 * 48, 36 * 48, 192, 96)
    block(2, lambda i, dy: w2[i, dy], b2, s2, 256, 192, 704, 20 * 32, 20 * 32, 160, 32)
    block(
        3,
        lambda i, dy: w3[i, :, dy * 1152 : (dy + 1) * 1152],
        b3, s3, 384, 384, 1152, 10 * 16, 10 * 16, 160, 16,
    )

    @pl.loop(0, 37)
    def _(r):
        for par in range(2):
            for dx in range(3):
                piece = a0[pl.ds((2 * r + par) * 80 + dx, 48, stride=2), 0:48]
                t0[par, pl.ds(pl.multiple_of(r * 48, 48), 48), dx * 64 : dx * 64 + 48] = piece.astype(BF)

    @pl.loop(0, 9)
    def _(i):
        p = pl.multiple_of(i * 192, 192)
        total = None
        for dy in range(3):
            part = dot_nt(t0[dy % 2, pl.ds(p + (dy // 2) * 48, 192), 0:192], d01[dy])
            total = part if total is None else total + part
        v01[pl.ds(p, 192), :] = rounded(total[:, :128])
        v0[pl.ds(p, 192), :] = rounded(jnp.maximum(total[:, 128:], 0.0))

    clear_edges(place, [v0], 48, 35, 35, 3, 0)

    @pl.loop(0, 18)
    def _(r):
        for par in range(2):
            for dx in range(3):
                piece = v0[pl.ds((2 * r + par) * 48 + dx, 32, stride=2), :]
                t02w[par, pl.ds(pl.multiple_of(r * 32, 32), 32), dx * 128 : dx * 128 + 128] = piece.astype(BF)
                piece = a1[pl.ds((2 * r + par) * 48 + dx, 32, stride=2), :]
                t1[par, pl.ds(pl.multiple_of(r * 32, 32), 32), dx * 128 : dx * 128 + 128] = piece.astype(BF)

    for p, n in ((0, 288), (288, 256)):
        total = other = None
        for dy in range(3):
            cut = pl.ds(p + (dy // 2) * 32, n)
            part = dot_nt(t02w[dy % 2, cut, :], d02[dy])
            total = part if total is None else total + part
            part = dot_nt(t1[dy % 2, cut, :], d12[dy])
            other = part if other is None else other + part
        vv02[0, p : p + n, :] = rounded(total[:, :128])
        vv02[1, p : p + n, 0:64] = rounded(total[:, 128:192])
        n03[p : p + n, :] = rounded(jnp.maximum(total[:, 192:240], 0.0))
        vv12[0, p : p + n, :] = rounded(other[:, :128])
        vv12[1, p : p + n, 0:64] = rounded(other[:, 128:192])
        m13[p : p + n, :] = rounded(jnp.maximum(other[:, 256:352], 0.0))

    clear_edges(place, [n03], 32, 17, 17, 1, 0)
    clear_edges(place, [m13], 32, 17, 17, 1, 0)

    def gathered(ref, width, dy, dx):
        return jnp.concatenate(
            [ref[pl.ds((2 * i + dy) * 32 + dx, 8, stride=2), 0:width] for i in range(8)], axis=0
        ).astype(BF)

    t03 = t13 = t23 = None
    for tap in range(9):
        dy, dx = divmod(tap, 3)
        part = dot_nt(gathered(n03, 48, dy, dx), fin03[tap])
        t03 = part if t03 is None else t03 + part
        part = dot_nt(gathered(m13, 96, dy, dx), fin13[tap])
        t13 = part if t13 is None else t13 + part
        for s, (lo, hi) in enumerate(spans(192)):
            part = jnp.dot(
                gathered(a2.at[s], hi - lo, dy, dx),
                fin23[tap * 192 + lo : tap * 192 + hi, :],
                preferred_element_type=F32,
            )
            t23 = part if t23 is None else t23 + part

    c3 = [
        jnp.concatenate([a3[s, y * 16 : y * 16 + 8, :] for y in range(8)], axis=0) for s in range(3)
    ]
    c3 = jnp.concatenate(c3, axis=1)
    three = jnp.maximum(c3 + rounded(t03) + rounded(t13) + rounded(t23), 0.0)
    j3[...] = three.reshape(8, 8, 384).astype(BF)

    c3b = c3.astype(BF)
    t30 = rounded(dot_nt(c3b, u3[0:48, :]))
    t31 = rounded(dot_nt(c3b, u3[48:144, :]))
    t32 = rounded(dot_nt(c3b, u3[144:336, :]))
    c2 = [
        jnp.concatenate([a2[s, pl.ds((y + 1) * 32 + 1, 16), 0 : hi - lo] for y in range(16)], axis=0)
        for s, (lo, hi) in enumerate(spans(192))
    ]
    c2 = jnp.concatenate(c2, axis=1)
    c2b = c2.astype(BF)
    t20 = rounded(dot_nt(c2b, u2[0:48, :]))
    t21 = rounded(dot_nt(c2b, u2[48:144, :]))

    def doubled(target, small, side, lanes):
        for y in range(side):
            row = small[y * side : (y + 1) * side]
            for odd in range(2):
                for right in range(2):
                    target[pl.ds((2 * y + odd) * 2 * side + right, side, stride=2), 0:lanes] = row

    for s, (lo, hi) in enumerate(spans(192)):
        doubled(wide, t32[:, lo:hi], 8, hi - lo)
        for y in range(16):
            t02 = vv02[s, pl.ds((y + 1) * 32 + 1, 16), 0 : hi - lo]
            t12 = vv12[s, pl.ds((y + 1) * 32 + 1, 16), 0 : hi - lo]
            keep = c2[y * 16 : (y + 1) * 16, lo:hi]
            row = keep + t02 + t12 + wide[pl.ds(y * 16, 16), 0 : hi - lo]
            j2[y, :, lo:hi] = jnp.maximum(row, 0.0).astype(BF)

    doubled(z2, t30, 8, 48)
    sum2 = z2[...] + t20
    doubled(z1, sum2, 16, 48)
    doubled(y2, t31, 8, 96)
    sum2 = y2[...] + t21
    doubled(y1, sum2, 16, 96)

    @pl.loop(0, 32)
    def _(y):
        one = a1[pl.ds((y + 3) * 48 + 3, 32), 0:96]
        t01 = v01[pl.ds((y + 3) * 48 + 3, 32), 0:96]
        spot = pl.ds(pl.multiple_of(y * 32, 32), 32)
        j1[y] = jnp.maximum(one + t01 + y1[spot, :], 0.0).astype(BF)
        row = rounded(dot_nt(one.astype(BF), u1[...])) + z1[spot, :]
        for right in range(2):
            mcol[pl.ds(right, 32, stride=2), :] = row
        for odd in range(2):
            zero = a0[pl.ds((2 * y + odd + 7) * 80 + 7, 64), 0:48]
            j0[2 * y + odd] = jnp.maximum(zero + mcol[...], 0.0).astype(BF)


def ring(x, axis, by):
    n = lax.axis_size(axis)
    return lax.ppermute(x, axis, [(i, (i + by) % n) for i in range(n)])


def shape(*dims, kind=BF):
    return jax.ShapeDtypeStruct(dims, kind)


def slotted(w, chan, slot):
    taps = w.reshape(w.shape[0], 3, 3, chan).transpose(1, 0, 2, 3)
    taps = jnp.pad(taps, ((0, 0), (0, 0), (0, 0), (0, slot - chan)))
    return taps.reshape(3, w.shape[0], 3 * slot)


def tapped(w, chan):
    return w.reshape(w.shape[0], 9, chan).transpose(1, 0, 2)


def padded_rows(w, rows):
    return jnp.pad(w, ((0, rows - w.shape[0]), (0, 0)))


def per_device(
    feat0, feat1, feat2, feat3,
    block_w0, block_w1, block_w2, block_w3,
    block_b0, block_b1, block_b2, block_b3,
    up_w1, up_w2, up_w3,
    down_mid0, down_mid1, down_fin0, down_fin1, down_fin2,
):
    maps = [f.transpose(1, 2, 0) for f in (feat0, feat1, feat2, feat3)]
    down, up = pl.pallas_call(
        pack_rows,
        out_shape=[shape(DOWN_ROWS, 128), shape(UP_ROWS, 128)],
        compiler_params=PARAMS,
    )(*maps)
    above, below = ring(down, "ty", 1), ring(up, "ty", -1)
    right, left = pl.pallas_call(
        pack_cols,
        out_shape=[shape(RIGHT_ROWS, 128), shape(LEFT_ROWS, 128)],
        scratch_shapes=[pltpu.VMEM((3, 80 * 16, 128), F32)],
        compiler_params=PARAMS,
    )(*maps, above, below)
    cl, cr = ring(right, "tx", 1), ring(left, "tx", -1)

    w0 = jnp.stack([slotted(block_w0[i], 48, 64) for i in range(2)])
    w1 = jnp.stack([slotted(block_w1[i], 96, 128) for i in range(2)])
    w2 = jnp.stack([slotted(block_w2[i], 192, 256)[:, :, :704] for i in range(2)])
    fin0, mid0 = down_fin0[0], down_mid0[0]
    d01 = slotted(
        jnp.concatenate(
            [padded_rows(fin0[:96], 128), padded_rows(mid0[0], 64), padded_rows(mid0[1], 64)]
        ),
        48,
        64,
    )
    taps = fin0[96:288].reshape(192, 9, 48)
    inner = mid0[2].reshape(48, 9, 48)
    d02 = jnp.concatenate(
        [
            jnp.pad(taps, ((0, 0), (0, 0), (0, 80))),
            jnp.pad(inner, ((0, 16), (0, 0), (64, 16))),
        ]
    ).reshape(256, 3, 384).transpose(1, 0, 2)
    d12 = slotted(
        jnp.concatenate([padded_rows(down_fin1[0, :192], 256), down_mid1[0, 0]]), 96, 128
    )
    fin03 = tapped(fin0[288:], 48)
    fin13 = tapped(down_fin1[0, 192:], 96)
    fin23 = down_fin2[0].T
    place = jnp.stack([lax.axis_index("ty"), lax.axis_index("tx")]).astype(jnp.int32)

    vmem = pl.BlockSpec(memory_space=pltpu.VMEM)
    f32 = lambda *dims: pltpu.VMEM(dims, F32)
    bf = lambda *dims: pltpu.VMEM(dims, BF)
    outs = pl.pallas_call(
        main,
        out_shape=[shape(64, 64, 48), shape(32, 32, 96), shape(16, 16, 192), shape(8, 8, 384)],
        in_specs=[pl.BlockSpec(memory_space=pltpu.SMEM)] + [vmem] * 25,
        scratch_shapes=[
            f32(6416, 48), f32(6320, 48), f32(6064, 48), bf(6400, 256), bf(2, 38 * 48, 192),
            f32(1728, 128), f32(1840, 128), bf(2, 19 * 32, 384), f32(2, 544, 128), f32(600, 48),
            f32(2080, 128), f32(2032, 128), f32(1840, 128), bf(2048, 384), bf(2, 19 * 32, 384),
            f32(2, 544, 128), f32(600, 96),
            f32(2, 768, 128), f32(2, 768, 128), f32(2, 704, 128), bf(768, 768),
            f32(3, 224, 128), f32(3, 224, 128), f32(3, 176, 128), bf(208, 1152),
            f32(1024, 48), f32(256, 48), f32(256, 96), f32(1024, 96), f32(256, 128), f32(64, 48),
        ],
        compiler_params=PARAMS,
    )(
        place, *maps, above, below, cl, cr,
        w0, w1, w2, block_w3, block_b0, block_b1, block_b2, block_b3,
        up_w1[0], up_w2[0], up_w3[0], d01, d02, d12, fin03, fin13, fin23,
    )
    return tuple(o.transpose(2, 0, 1) for o in outs)


def solution(mesh):
    tile = P(None, "ty", "tx")
    return jax.shard_map(
        per_device,
        mesh=mesh,
        in_specs=(tile,) * 4 + (P(),) * 16,
        out_specs=(tile,) * 4,
        check_vma=False,
    )
```

profile of v0, /device:TPU:4, one launch (start us, length us, event | category | flops | bytes accessed | tf_op | source)
XLA Modules:
  0.0 98.4 jit_solution(4272490334337918428)
XLA Ops:
  0.6 2.8 %copy.38 = bf16[48,64,64]{0,2,1:T(8,128)(2,1)} copy(bf16[48,64,64]{2,1,0:T(8,128)(2,1)} %param.20) | data formatting | bytes 786432 | tf_op args[0]
  3.4 2.2 %shard_map.219 = (bf16[592,128]{1,0:T(8,128)(2,1)}, bf16[240,128]{1,0:T(8,128)(2,1)}) custom-call(bf16[64,64,48]{2,1,0:T(8,128)(2,1)} %bitcast.62, bf16[32,32,96]{2,1,0:T(8,128)(2,1)} %bitcast.75, bf16[16,16,192]{2,1,0:T(8,128)(2,1)} %bitcast.84, bf16[8,8,384]{2,1,0:T(8,128)(2,1)} %bitcast.98), custom_call_target="tpu_custom_call" | custom-call | tf_op jit(solution)/shard_map/pallas_call | solution.py:403
  5.6 1.6 %collective-permute-start = (bf16[592,128]{1,0:T(8,128)(2,1)}, bf16[592,128]{1,0:T(8,128)(2,1)}, u32[]{:S(2)}, u32[]{:S(2)}) collective-permute-start(bf16[592,128]{1,0:T(8,128)(2,1)} %get-tuple-element.12), channel_id=1, source_target_pairs={{0,8},{8,16},{16,24},{24,32},{32,40},{40,48},{48,56},{56,0},{1,9},... | collective-permute-start | bytes 454664 | tf_op jit(solution)/shard_map/ppermute | solution.py:374
  7.2 2.6 %collective-permute-start.1 = (bf16[240,128]{1,0:T(8,128)(2,1)}, bf16[240,128]{1,0:T(8,128)(2,1)}, u32[]{:S(2)}, u32[]{:S(2)}) collective-permute-start(bf16[240,128]{1,0:T(8,128)(2,1)} %get-tuple-element.13), channel_id=1, source_target_pairs={{0,56},{8,0},{16,8},{24,16},{32,24},{40,32},{48,40},{56,48},{1,57}... | collective-permute-start | bytes 184328 | tf_op jit(solution)/shard_map/ppermute | solution.py:374
  9.9 0.6 fusion.11
  10.6 0.3 copy.69
  11.2 0.8 copy.70
  12.0 0.3 copy.71
  12.6 0.8 copy.72
  13.4 1.8 %fusion.10 = (bf16[1,96,864]{2,1,0:T(8,128)(2,1)}, bf16[1,96,864]{2,1,0:T(8,128)(2,1)}) fusion(bf16[2,96,864]{2,1,0:T(8,128)(2,1)} %param.25), kind=kLoop, calls=%fused_computation.22 | loop fusion | bytes 663552 | tf_op jit(solution)/shard_map/slice | solution.py:418
  15.2 0.9 copy.75
  16.2 1.5 %fusion.12 = (bf16[1,48,432]{2,1,0:T(8,128)(2,1)}, bf16[1,48,432]{2,1,0:T(8,128)(2,1)}) fusion(bf16[2,48,432]{2,1,0:T(8,128)(2,1)} %param.24), kind=kLoop, calls=%fused_computation.24 | loop fusion | bytes 165888 | tf_op jit(solution)/shard_map/slice | solution.py:417
  17.6 0.2 copy.76
  17.9 1.1 %copy.54 = bf16[1,1,96,864]{2,3,1,0:T(8,128)(2,1)S(1)} copy(bf16[1,1,96,864]{3,2,1,0:T(8,128)(2,1)} %param.36) | data formatting | bytes 331776 | tf_op args[16]
  19.0 1.4 %pad_maximum_fusion.w2 = bf16[2,3,192,704]{3,2,1,0:T(8,128)(2,1)} fusion(bf16[1,3,192,704]{3,2,1,0:T(8,128)(2,1)S(1)} %bitcast.68, bf16[1,3,192,704]{3,2,1,0:T(8,128)(2,1)S(1)} %bitcast.67), kind=kLoop, calls=%fused_computation | loop fusion | flops 811008 | bytes 3244032 | tf_op jit(solution)/shard_map/stack | solution.py:419
  20.6 0.6 copy-done.7
  22.5 2.6 %shard_map.220 = (bf16[928,128]{1,0:T(8,128)(2,1)}, bf16[400,128]{1,0:T(8,128)(2,1)}) custom-call(bf16[64,64,48]{2,1,0:T(8,128)(2,1)} %bitcast.63, bf16[32,32,96]{2,1,0:T(8,128)(2,1)} %bitcast.76, bf16[16,16,192]{2,1,0:T(8,128)(2,1)} %bitcast.85, bf16[8,8,384]{2,1,0:T(8,128)(2,1)} %bitcast.99, bf16[592,128]{1,0:T(8,128)(2,1)} %collective-permute-done.above, ...), custom_call_target="tpu_custom_call" | custom-call | tf_op jit(solution)/shard_map/pallas_call | solution.py:409
  25.1 1.9 %collective-permute-start.2 = (bf16[928,128]{1,0:T(8,128)(2,1)}, bf16[928,128]{1,0:T(8,128)(2,1)S(1)}, u32[]{:S(2)}, u32[]{:S(2)}) collective-permute-start(bf16[928,128]{1,0:T(8,128)(2,1)} %get-tuple-element.14), channel_id=1, source_target_pairs={{0,1},{1,2},{2,3},{3,4},{4,5},{5,6},{6,7},{7,0},{8,9},{9,10},{10,1... | collective-permute-start | bytes 712712 | tf_op jit(solution)/shard_map/ppermute | solution.py:374
  27.0 0.7 pad_maximum_fusion.2.w0
  27.9 0.9 copy.58.d01
  29.7 1.1 %copy.52 = bf16[256,3,384]{2,0,1:T(8,128)(2,1)} copy(bf16[256,3,384]{0,2,1:T(8,128)(2,1)S(1)} %bitcast.79) | data formatting | bytes 1179648 | tf_op jit(solution)/shard_map/reshape | solution.py:435
  30.9 2.1 %copy.59.d12 = bf16[3,352,384]{2,1,0:T(8,128)(2,1)} copy(bf16[3,352,384]{1,2,0:T(8,128)(2,1)S(1)} %bitcast.71) | data formatting | bytes 1622016 | tf_op jit(solution)/shard_map/reshape | solution.py:384
  33.0 0.3 copy.77
  33.4 1.3 %copy.57 = bf16[384,9,96]{2,0,1:T(8,128)(2,1)} copy(bf16[384,9,96]{0,2,1:T(8,128)(2,1)S(1)} %bitcast.74) | data formatting | bytes 1327104 | tf_op jit(solution)/shard_map/reshape;squeeze | solution.py:388
  34.7 1.2 %copy.55 = bf16[384,9,48]{2,0,1:T(8,128)(2,1)} copy(bf16[384,9,48]{0,2,1:T(8,128)(2,1)S(1)} %bitcast.83) | data formatting | bytes 663552 | tf_op jit(solution)/shard_map/reshape | solution.py:388
  35.9 0.8 pad_maximum_fusion.1.w1
  36.7 3.9 %collective-permute-start.3 = (bf16[400,128]{1,0:T(8,128)(2,1)S(1)}, bf16[400,128]{1,0:T(8,128)(2,1)S(1)}, u32[]{:S(2)}, u32[]{:S(2)}) collective-permute-start(bf16[400,128]{1,0:T(8,128)(2,1)S(1)} %copy-done.12), channel_id=1, source_target_pairs={{0,7},{1,0},{2,1},{3,2},{4,3},{5,4},{6,5},{7,6},{8,15},{9,8},{10,9... | collective-permute-start | bytes 307208 | tf_op jit(solution)/shard_map/ppermute | solution.py:374
  40.7 0.6 pad_add_fusion.place
  41.3 1.6 %collective-permute-done.3.cr = bf16[400,128]{1,0:T(8,128)(2,1)S(1)} collective-permute-done((bf16[400,128]{1,0:T(8,128)(2,1)S(1)}, bf16[400,128]{1,0:T(8,128)(2,1)S(1)}, u32[]{:S(2)}, u32[]{:S(2)}) %collective-permute-start.3) | collective-permute-done | bytes 102432 | tf_op jit(solution)/shard_map/ppermute | solution.py:374
  42.9 0.6 copy-done.11
  43.7 51.8 %shard_map.221 = (bf16[64,64,48]{2,1,0:T(8,128)(2,1)}, bf16[32,32,96]{2,1,0:T(8,128)(2,1)}, bf16[16,16,192]{2,1,0:T(8,128)(2,1)}, bf16[8,8,384]{2,1,0:T(8,128)(2,1)}) custom-call(s32[2]{0:T(128)} %pad_add_fusion.place, bf16[64,64,48]{2,1,0:T(8,128)(2,1)} %bitcast.64, bf16[32,32,96]{2,1,0:T(8,128)(2,1)} %bitcast.77, bf16[16,16,192]{2,1,0:T(8,128)(2,1)} %bitcast.86, ...), custom_call_target="tpu_custom_call" | custom-call | tf_op jit(solution)/shard_map/pallas_call | solution.py:447
  95.5 2.9 %copy.60 = bf16[48,64,64]{2,1,0:T(8,128)(2,1)} copy(bf16[48,64,64]{0,2,1:T(8,128)(2,1)} %bitcast.90) | data formatting | bytes 786432
  (61 shorter events, 3.4 us)
Async XLA Ops:
  0.6 9.1 %copy-start.3 = (bf16[1,672,432]{1,2,0:T(8,128)(2,1)S(1)}, bf16[1,672,432]{1,2,0:T(8,128)(2,1)}, u32[]{:S(2)}) copy-start(bf16[1,672,432]{1,2,0:T(8,128)(2,1)} %param.37) | copy-start | bytes 1741828
  3.4 6.5 %copy-start.10 = (bf16[1,3,48,432]{3,2,1,0:T(8,128)(2,1)S(1)}, bf16[1,3,48,432]{3,2,1,0:T(8,128)(2,1)}, u32[]{:S(2)}) copy-start(bf16[1,3,48,432]{3,2,1,0:T(8,128)(2,1)} %param.35) | copy-start | bytes 373252
  3.4 7.2 %copy-start = (bf16[2,192,1728]{2,1,0:T(8,128)(2,1)S(1)}, bf16[2,192,1728]{2,1,0:T(8,128)(2,1)}, u32[]{:S(2)}) copy-start(bf16[2,192,1728]{2,1,0:T(8,128)(2,1)} %param.26) | copy-start | bytes 3981316
  5.6 16.9 %collective-permute-start = (bf16[592,128]{1,0:T(8,128)(2,1)}, bf16[592,128]{1,0:T(8,128)(2,1)}, u32[]{:S(2)}, u32[]{:S(2)}) collective-permute-start(bf16[592,128]{1,0:T(8,128)(2,1)} %get-tuple-element.12), channel_id=1, source_target_pairs={{0,8},{8,16},{16,24},{24,32},{32,40},{40,48},{48,56},{56,0},{1,9},... | collective-permute-start | bytes 454664 | tf_op jit(solution)/shard_map/ppermute | solution.py:374
  7.2 15.3 %collective-permute-start.1 = (bf16[240,128]{1,0:T(8,128)(2,1)}, bf16[240,128]{1,0:T(8,128)(2,1)}, u32[]{:S(2)}, u32[]{:S(2)}) collective-permute-start(bf16[240,128]{1,0:T(8,128)(2,1)} %get-tuple-element.13), channel_id=1, source_target_pairs={{0,56},{8,0},{16,8},{24,16},{32,24},{40,32},{48,40},{56,48},{1,57}... | collective-permute-start | bytes 184328 | tf_op jit(solution)/shard_map/ppermute | solution.py:374
  13.4 4.2 %slice-start = ((bf16[1,576,864]{2,1,0:T(8,128)(2,1)}), bf16[1,192,864]{2,1,0:T(8,128)(2,1)S(1)}, s32[]{:S(2)}) async-start(bf16[1,576,864]{2,1,0:T(8,128)(2,1)} %param.38), calls=%async_computation | async-start | bytes 688128 | tf_op jit(solution)/shard_map/slice | solution.py:437
  20.4 0.8 copy-start.7
  20.4 0.9 copy-start.6
  20.4 1.1 %copy-start.9 = (bf16[1,48,432]{2,1,0:T(8,128)(2,1)S(1)}, bf16[1,48,432]{2,1,0:T(8,128)(2,1)}, u32[]{:S(2)}) copy-start(bf16[1,48,432]{2,1,0:T(8,128)(2,1)} %get-tuple-element.35) | copy-start | bytes 124420
  20.5 1.4 %copy-start.8 = (bf16[1,48,432]{2,1,0:T(8,128)(2,1)S(1)}, bf16[1,48,432]{2,1,0:T(8,128)(2,1)}, u32[]{:S(2)}) copy-start(bf16[1,48,432]{2,1,0:T(8,128)(2,1)} %get-tuple-element.36) | copy-start | bytes 124420
  22.5 5.2 %copy-start.4 = (bf16[1,672,432]{1,2,0:T(8,128)(2,1)S(1)}, bf16[1,672,432]{1,2,0:T(8,128)(2,1)}, u32[]{:S(2)}) copy-start(bf16[1,672,432]{1,2,0:T(8,128)(2,1)} %param.37) | copy-start | bytes 1741828
  25.1 17.8 %collective-permute-start.2 = (bf16[928,128]{1,0:T(8,128)(2,1)}, bf16[928,128]{1,0:T(8,128)(2,1)S(1)}, u32[]{:S(2)}, u32[]{:S(2)}) collective-permute-start(bf16[928,128]{1,0:T(8,128)(2,1)} %get-tuple-element.14), channel_id=1, source_target_pairs={{0,1},{1,2},{2,3},{3,4},{4,5},{5,6},{6,7},{7,0},{8,9},{9,10},{10,1... | collective-permute-start | bytes 712712 | tf_op jit(solution)/shard_map/ppermute | solution.py:374
  27.7 1.1 %copy-start.2 = (bf16[1,96,864]{2,1,0:T(8,128)(2,1)S(1)}, bf16[1,96,864]{2,1,0:T(8,128)(2,1)}, u32[]{:S(2)}) copy-start(bf16[1,96,864]{2,1,0:T(8,128)(2,1)} %get-tuple-element.30) | copy-start | bytes 497668
  27.9 1.4 %copy-start.1 = (bf16[1,96,864]{2,1,0:T(8,128)(2,1)S(1)}, bf16[1,96,864]{2,1,0:T(8,128)(2,1)}, u32[]{:S(2)}) copy-start(bf16[1,96,864]{2,1,0:T(8,128)(2,1)} %get-tuple-element.31) | copy-start | bytes 497668
  30.8 2.3 %slice-start.1 = ((bf16[1,576,864]{2,1,0:T(8,128)(2,1)}), bf16[1,384,864]{2,1,0:T(8,128)(2,1)S(1)}, s32[]{:S(2)}) async-start(bf16[1,576,864]{2,1,0:T(8,128)(2,1)} %param.38), calls=%async_computation.1 | async-start | bytes 1376256 | tf_op jit(solution)/shard_map/slice | solution.py:440
  34.7 2.1 %copy-start.12 = (bf16[400,128]{1,0:T(8,128)(2,1)S(1)}, bf16[400,128]{1,0:T(8,128)(2,1)}, u32[]{:S(2)}) copy-start(bf16[400,128]{1,0:T(8,128)(2,1)} %get-tuple-element.15) | copy-start | bytes 307204
  36.7 6.2 %collective-permute-start.3 = (bf16[400,128]{1,0:T(8,128)(2,1)S(1)}, bf16[400,128]{1,0:T(8,128)(2,1)S(1)}, u32[]{:S(2)}, u32[]{:S(2)}) collective-permute-start(bf16[400,128]{1,0:T(8,128)(2,1)S(1)} %copy-done.12), channel_id=1, source_target_pairs={{0,7},{1,0},{2,1},{3,2},{4,3},{5,4},{6,5},{7,6},{8,15},{9,8},{10,9... | collective-permute-start | bytes 307208 | tf_op jit(solution)/shard_map/ppermute | solution.py:374
  42.9 0.7 copy-start.11
  42.9 0.7 copy-start.5
where the time goes:
time: 99 us; the launch traced here: 98.4 us
  Pallas kernels  56.6 us (57%)
  local copies, waits for them, and re-layouts  25.3 us (26%)
  starting transfers between devices  9.99 us (10%)
  other arithmetic  3.87 us (4%)
  waiting for transfers between devices  1.62 us (2%)
    pallas_call x1, Pallas kernels, per_device(): pl.pallas_call(main, out_shape=[shape(64, 64, 48), shape(32, 32, 96), sha...  51.8 us
    unnamed x40, local copies, waits for them, and re-layouts  12.4 us
    ppermute x4, starting transfers between devices, ring(): return lax.ppermute(x, axis, [(i, (i + by) % n) for i in range(n)])  9.99 us
    reshape x2, local copies, waits for them, and re-layouts, slotted(): return taps.reshape(3, w.shape[0], 3 * slot)  3.05 us
    pallas_call x1, Pallas kernels, per_device(): pl.pallas_call(pack_cols, out_shape=[shape(RIGHT_ROWS, 128), shape(LEFT_R...  2.6 us
    pallas_call x1, Pallas kernels, per_device(): pl.pallas_call(pack_rows, out_shape=[shape(DOWN_ROWS, 128), shape(UP_ROWS...  2.2 us
  transfers between devices with their start and end apart: 4, of which 1 were waited for; matrix products, arithmetic and copies ran while one was open for 23% of the time, Pallas kernels for 0%

commit v1 on v0

--- a/solution.py
+++ b/solution.py
@@ -18,7 +18,8 @@
 GROUP = (16, 16, 16, 8)
 DOWN_ROWS, UP_ROWS = 592, 240
 RIGHT_ROWS, LEFT_ROWS = 928, 400
-PARAMS = pltpu.CompilerParams(vmem_limit_bytes=56 * 2**20)
+PARAMS = pltpu.CompilerParams(vmem_limit_bytes=16 * 2**20)
+MAIN_PARAMS = pltpu.CompilerParams(vmem_limit_bytes=56 * 2**20)
 
 
 def spans(chan):
@@ -136,25 +137,34 @@
 
 
 def main(
-    place, f0, f1, f2, f3, above, below, cl, cr,
-    w0, w1, w2, w3, b0, b1, b2, b3, u1, u2, u3, d01, d02, d12, fin03, fin13, fin23,
+    f0, f1, f2, f3, above, below, cl, cr,
+    w0, b0, b1, b2, b3, u1, *rest,
+):
+    far, rest = rest[:10], rest[10:]
+    outs, near, scratch = rest[:4], rest[4:14], rest[14:-1]
+    main_body(
+        f0, f1, f2, f3, above, below, cl, cr, w0, b0, b1, b2, b3, u1, far, near, rest[-1], *outs, *scratch
+    )
+
+
+def main_body(
+    f0, f1, f2, f3, above, below, cl, cr, w0, b0, b1, b2, b3, u1, far, near, sems,
     j0, j1, j2, j3,
-    x0, h0, a0, s0, t0, v01, v0, t02w, vv02, n03,
-    x1, h1, a1, s1, t1, vv12, m13,
-    x2, h2, a2, s2,
+    x0, h0, a0, s0, t0, d01, v01, v0, ta, tb, vv02, n03, g03,
+    x1, h1, a1, s1, t1, vv12, m13, g13,
+    x2, h2, a2, s2, g23,
     x3, h3, a3, s3,
-    z1, z2, y2, y1, wide, mcol,
+    z1, z2, y2, y1, wide, c1, mcol, jt,
 ):
+    place = (lax.axis_index("ty"), lax.axis_index("tx"))
+    copies = [pltpu.make_async_copy(a, b, sems.at[i]) for i, (a, b) in enumerate(zip(far, near))]
+    for copy in copies:
+        copy.start()
+    w1, w2, w3, mid0, mid1, fin0, fin1, fin2, u3, u2 = near
     feats = (f0, f1, f2, f3)
     xs = ([x0], [x1], [x2.at[0], x2.at[1]], [x3.at[i] for i in range(3)])
     hs = ([h0], [h1], [h2.at[0], h2.at[1]], [h3.at[i] for i in range(3)])
     as_ = ([a0], [a1], [a2.at[0], a2.at[1]], [a3.at[i] for i in range(3)])
-    x1[:, 96:128] = jnp.zeros((x1.shape[0], 32), F32)
-    h1[:, 96:128] = jnp.zeros((h1.shape[0], 32), F32)
-    a1[:, 96:128] = jnp.zeros((a1.shape[0], 32), F32)
-    s0[...] = jnp.zeros_like(s0)
-    t0[...] = jnp.zeros_like(t0)
-    s2[...] = jnp.zeros_like(s2)
 
     def assemble(b, ats):
         side, lead, chan, pitch = TILE[b], LEAD[b], CHAN[b], PITCH[b]
@@ -196,98 +206,120 @@
     for b in range(4):
         ats = assemble(b, ats)
 
-    def spread(planes, target, rows, step, slot, chan, lanes):
-        @pl.loop(0, rows // step)
+    def steps(rows, count, body):
+        step = rows // count
+        if count == 1:
+            body(0, step)
+            return
+
+        @pl.loop(0, count)
         def _(i):
-            p = pl.multiple_of(i * step, step)
+            body(pl.multiple_of(i * step, 16), step)
+
+    def spread(planes, target, rows, count, chan):
+        def body(p, step):
             for dx in range(3):
-                for s, (lo, hi) in enumerate(spans(lanes)):
+                for s, (lo, hi) in enumerate(spans(chan)):
                     piece = planes[s][pl.ds(p + dx, step), 0 : hi - lo].astype(BF)
-                    target[pl.ds(p, step), dx * slot + lo : dx * slot + hi] = piece
-
-    def conv_loop(source, weight, rows, step, pitch, width, finish):
-        @pl.loop(0, rows // step)
-        def _(i):
-            p = pl.multiple_of(i * step, step)
+                    target[pl.ds(p, step), dx * chan + lo : dx * chan + hi] = piece
+
+        steps(rows, count, body)
+
+    def block(b, weight, bias, source, counts):
+        pitch, chan, lead = PITCH[b], CHAN[b], LEAD[b]
+        width = 3 * chan
+
+        def conv(i, p, step):
             total = None
             for dy in range(3):
-                part = dot_nt(source[pl.ds(p + dy * pitch, step), 0:width], weight(dy))
+                part = dot_nt(
+                    source[pl.ds(p + dy * pitch, step), :],
+                    weight[i, :, dy * width : (dy + 1) * width],
+                )
                 total = part if total is None else total + part
-            finish(p, total)
-
-    def block(b, weight, bias, source, slot, lanes, width, inner_rows, outer_rows, step, copy_step):
-        pitch, chan, lead = PITCH[b], CHAN[b], LEAD[b]
-
-        def inner(p, total):
-            value = jnp.maximum(total + bias[0:1, :], 0.0)
+            return total + bias[i : i + 1, :]
+
+        def inner(p, step):
+            value = jnp.maximum(conv(0, p, step), 0.0)
             for s, (lo, hi) in enumerate(spans(chan)):
                 hs[b][s][pl.ds(p, step), 0 : hi - lo] = value[:, lo:hi]
 
-        def outer(p, total):
-            total = total + bias[1:2, :]
+        def outer(p, step):
+            total = conv(1, p, step)
             for s, (lo, hi) in enumerate(spans(chan)):
                 kept = xs[b][s][pl.ds(p + 2 * pitch + 2, step), 0 : hi - lo]
                 value = rounded(jnp.maximum(kept + total[:, lo:hi], 0.0))
                 as_[b][s][pl.ds(p, step), 0 : hi - lo] = value
 
-        spread(xs[b], source, inner_rows + 2 * pitch, copy_step, slot, chan, lanes)
-        conv_loop(source, lambda dy: weight(0, dy), inner_rows, step, pitch, width, inner)
+        inner_rows, outer_rows = (EXT[b] - 2) * pitch, (EXT[b] - 4) * pitch
+        spread(xs[b], source, inner_rows + 2 * pitch, counts[0], chan)
+        steps(inner_rows, counts[1], inner)
         clear_edges(place, hs[b], pitch, EXT[b] - 2, EXT[b] - 2, lead - 1, 1)
-        spread(hs[b], source, outer_rows + 2 * pitch, copy_step, slot, chan, lanes)
-        conv_loop(source, lambda dy: weight(1, dy), outer_rows, step, pitch, width, outer)
+        spread(hs[b], source, outer_rows + 2 * pitch, counts[2], chan)
+        steps(outer_rows, counts[3], outer)
         clear_edges(place, as_[b], pitch, EXT[b] - 4, EXT[b] - 4, lead - 2, 0)
 
-    block(0, lambda i, dy: w0[i, dy], b0, s0, 64, 48, 192, 76 * 80, 72 * 80, 320, 160)
-    block(1, lambda i, dy: w1[i, dy], b1, s1, 128, 128, 384, 40 * 48, 36 * 48, 192, 96)
-    block(2, lambda i, dy: w2[i, dy], b2, s2, 256, 192, 704, 20 * 32, 20 * 32, 160, 32)
-    block(
-        3,
-        lambda i, dy: w3[i, :, dy * 1152 : (dy + 1) * 1152],
-        b3, s3, 384, 384, 1152, 10 * 16, 10 * 16, 160, 16,
-    )
-
-    @pl.loop(0, 37)
-    def _(r):
-        for par in range(2):
-            for dx in range(3):
-                piece = a0[pl.ds((2 * r + par) * 80 + dx, 48, stride=2), 0:48]
-                t0[par, pl.ds(pl.multiple_of(r * 48, 48), 48), dx * 64 : dx * 64 + 48] = piece.astype(BF)
-
-    @pl.loop(0, 9)
-    def _(i):
-        p = pl.multiple_of(i * 192, 192)
+    block(0, w0, b0, s0, (5, 5, 5, 5))
+    copies[0].wait()
+    block(1, w1, b1, s1, (3, 3, 3, 3))
+    copies[1].wait()
+    block(2, w2, b2, s2, (1, 2, 1, 2))
+    copies[2].wait()
+    block(3, w3, b3, s3, (1, 1, 1, 1))
+
+    for copy in copies[3:]:
+        copy.wait()
+    d01[...] = jnp.zeros_like(d01)
+    d01[0:96, :] = fin0[0:96, :]
+    d01[128:176, :] = mid0[0]
+    d01[192:240, :] = mid0[1]
+
+    def halve(source, lane, chan, target, row, pitch, count):
+        for dx in range(3):
+            piece = source[pl.ds(row * pitch + dx, count, stride=2), :][:, lane : lane + chan]
+            spot = pl.ds(row // 2 * count, count)
+            target[row % 2, spot, dx * chan : (dx + 1) * chan] = piece.astype(BF)
+
+    for row in range(71):
+        halve(a0, 0, 48, t0, row, 80, 48)
+
+    def first(p, step):
         total = None
         for dy in range(3):
-            part = dot_nt(t0[dy % 2, pl.ds(p + (dy // 2) * 48, 192), 0:192], d01[dy])
+            part = dot_nt(
+                t0[dy % 2, pl.ds(p + (dy // 2) * 48, step), :], d01[:, dy * 144 : (dy + 1) * 144]
+            )
             total = part if total is None else total + part
-        v01[pl.ds(p, 192), :] = rounded(total[:, :128])
-        v0[pl.ds(p, 192), :] = rounded(jnp.maximum(total[:, 128:], 0.0))
-
+        v01[pl.ds(p, step), :] = rounded(total[:, :128])
+        v0[pl.ds(p, step), :] = rounded(jnp.maximum(total[:, 128:], 0.0))
+
+    steps(35 * 48, 5, first)
     clear_edges(place, [v0], 48, 35, 35, 3, 0)
 
-    @pl.loop(0, 18)
-    def _(r):
-        for par in range(2):
-            for dx in range(3):
-                piece = v0[pl.ds((2 * r + par) * 48 + dx, 32, stride=2), :]
-                t02w[par, pl.ds(pl.multiple_of(r * 32, 32), 32), dx * 128 : dx * 128 + 128] = piece.astype(BF)
-                piece = a1[pl.ds((2 * r + par) * 48 + dx, 32, stride=2), :]
-                t1[par, pl.ds(pl.multiple_of(r * 32, 32), 32), dx * 128 : dx * 128 + 128] = piece.astype(BF)
-
-    for p, n in ((0, 288), (288, 256)):
-        total = other = None
+    for row in range(35):
+        halve(v0, 0, 48, ta, row, 48, 32)
+        halve(v0, 64, 48, tb, row, 48, 32)
+        halve(a1, 0, 96, t1, row, 48, 32)
+
+    def second(source, p, n, weight):
+        total = None
         for dy in range(3):
-            cut = pl.ds(p + (dy // 2) * 32, n)
-            part = dot_nt(t02w[dy % 2, cut, :], d02[dy])
+            part = dot_nt(source[dy % 2, p + dy // 2 * 32 : p + dy // 2 * 32 + n, :], weight(dy))
             total = part if total is None else total + part
-            part = dot_nt(t1[dy % 2, cut, :], d12[dy])
-            other = part if other is None else other + part
-        vv02[0, p : p + n, :] = rounded(total[:, :128])
-        vv02[1, p : p + n, 0:64] = rounded(total[:, 128:192])
-        n03[p : p + n, :] = rounded(jnp.maximum(total[:, 192:240], 0.0))
-        vv12[0, p : p + n, :] = rounded(other[:, :128])
-        vv12[1, p : p + n, 0:64] = rounded(other[:, 128:192])
-        m13[p : p + n, :] = rounded(jnp.maximum(other[:, 256:352], 0.0))
+        return total
+
+    for p, n in ((0, 272), (272, 272)):
+        cut = slice(p, p + n)
+        total = rounded(second(ta, p, n, lambda dy: fin0[96:288, dy * 144 : (dy + 1) * 144]))
+        vv02[0, cut, :] = total[:, :128]
+        vv02[1, cut, 0:64] = total[:, 128:192]
+        total = second(tb, p, n, lambda dy: mid0[2, :, dy * 144 : (dy + 1) * 144])
+        n03[cut, :] = rounded(jnp.maximum(total, 0.0))
+        total = rounded(second(t1, p, n, lambda dy: fin1[0:192, dy * 288 : (dy + 1) * 288]))
+        vv12[0, cut, :] = total[:, :128]
+        vv12[1, cut, 0:64] = total[:, 128:192]
+        total = second(t1, p, n, lambda dy: mid1[:, dy * 288 : (dy + 1) * 288])
+        m13[cut, :] = rounded(jnp.maximum(total, 0.0))
 
     clear_edges(place, [n03], 32, 17, 17, 1, 0)
     clear_edges(place, [m13], 32, 17, 17, 1, 0)
@@ -297,20 +329,15 @@
             [ref[pl.ds((2 * i + dy) * 32 + dx, 8, stride=2), 0:width] for i in range(8)], axis=0
         ).astype(BF)
 
-    t03 = t13 = t23 = None
     for tap in range(9):
         dy, dx = divmod(tap, 3)
-        part = dot_nt(gathered(n03, 48, dy, dx), fin03[tap])
-        t03 = part if t03 is None else t03 + part
-        part = dot_nt(gathered(m13, 96, dy, dx), fin13[tap])
-        t13 = part if t13 is None else t13 + part
+        g03[:, tap * 48 : tap * 48 + 48] = gathered(n03, 48, dy, dx)
+        g13[:, tap * 96 : tap * 96 + 96] = gathered(m13, 96, dy, dx)
         for s, (lo, hi) in enumerate(spans(192)):
-            part = jnp.dot(
-                gathered(a2.at[s], hi - lo, dy, dx),
-                fin23[tap * 192 + lo : tap * 192 + hi, :],
-                preferred_element_type=F32,
-            )
-            t23 = part if t23 is None else t23 + part
+            g23[:, tap * 192 + lo : tap * 192 + hi] = gathered(a2.at[s], hi - lo, dy, dx)
+    t03 = dot_nt(g03[...], fin0[288:672, :])
+    t13 = dot_nt(g13[...], fin1[192:576, :])
+    t23 = jnp.dot(g23[...], fin2[...], preferred_element_type=F32)
 
     c3 = [
         jnp.concatenate([a3[s, y * 16 : y * 16 + 8, :] for y in range(8)], axis=0) for s in range(3)
@@ -355,18 +382,34 @@
     sum2 = y2[...] + t21
     doubled(y1, sum2, 16, 96)
 
-    @pl.loop(0, 32)
-    def _(y):
-        one = a1[pl.ds((y + 3) * 48 + 3, 32), 0:96]
-        t01 = v01[pl.ds((y + 3) * 48 + 3, 32), 0:96]
-        spot = pl.ds(pl.multiple_of(y * 32, 32), 32)
-        j1[y] = jnp.maximum(one + t01 + y1[spot, :], 0.0).astype(BF)
-        row = rounded(dot_nt(one.astype(BF), u1[...])) + z1[spot, :]
-        for right in range(2):
-            mcol[pl.ds(right, 32, stride=2), :] = row
-        for odd in range(2):
-            zero = a0[pl.ds((2 * y + odd + 7) * 80 + 7, 64), 0:48]
-            j0[2 * y + odd] = jnp.maximum(zero + mcol[...], 0.0).astype(BF)
+    for y in range(32):
+        c1[y * 32 : y * 32 + 32, :] = a1[pl.ds((y + 3) * 48 + 3, 32), 0:96].astype(BF)
+    z1[...] += rounded(dot_nt(c1[...], u1[...]))
+
+    @pl.loop(0, 8)
+    def _(i):
+        for y in range(4):
+            y = 4 * i + y
+            spot = pl.ds(pl.multiple_of(y * 32, 32), 32)
+            one = a1[pl.ds((y + 3) * 48 + 3, 32), 0:96]
+            t01 = v01[pl.ds((y + 3) * 48 + 3, 32), 0:96]
+            j1[y] = jnp.maximum(one + t01 + y1[spot, :], 0.0).astype(BF)
+            spread_row = mcol.at[y % 4]
+            for right in range(2):
+                spread_row[pl.ds(right, 32, stride=2), :] = z1[spot, :]
+            pair = [
+                jnp.maximum(a0[pl.ds((2 * y + odd + 7) * 80 + 7, 64), :] + spread_row[...], 0.0)
+                for odd in range(2)
+            ]
+            turned = jnp.concatenate(pair, axis=0).T
+            for odd in range(2):
+                jt[pl.ds(2 * y + odd, 48, stride=64), :] = turned[:, odd * 64 : odd * 64 + 64]
+
+    @pl.loop(0, 6)
+    def _(i):
+        for c in range(8):
+            c = 8 * i + c
+            j0[c] = jt[pl.ds(pl.multiple_of(c * 64, 64), 64), :].astype(BF)
 
 
 def ring(x, axis, by):
@@ -376,20 +419,6 @@
 
 def shape(*dims, kind=BF):
     return jax.ShapeDtypeStruct(dims, kind)
-
-
-def slotted(w, chan, slot):
-    taps = w.reshape(w.shape[0], 3, 3, chan).transpose(1, 0, 2, 3)
-    taps = jnp.pad(taps, ((0, 0), (0, 0), (0, 0), (0, slot - chan)))
-    return taps.reshape(3, w.shape[0], 3 * slot)
-
-
-def tapped(w, chan):
-    return w.reshape(w.shape[0], 9, chan).transpose(1, 0, 2)
-
-
-def padded_rows(w, rows):
-    return jnp.pad(w, ((0, rows - w.shape[0]), (0, 0)))
 
 
 def per_device(
@@ -414,56 +443,35 @@
     )(*maps, above, below)
     cl, cr = ring(right, "tx", 1), ring(left, "tx", -1)
 
-    w0 = jnp.stack([slotted(block_w0[i], 48, 64) for i in range(2)])
-    w1 = jnp.stack([slotted(block_w1[i], 96, 128) for i in range(2)])
-    w2 = jnp.stack([slotted(block_w2[i], 192, 256)[:, :, :704] for i in range(2)])
-    fin0, mid0 = down_fin0[0], down_mid0[0]
-    d01 = slotted(
-        jnp.concatenate(
-            [padded_rows(fin0[:96], 128), padded_rows(mid0[0], 64), padded_rows(mid0[1], 64)]
-        ),
-        48,
-        64,
-    )
-    taps = fin0[96:288].reshape(192, 9, 48)
-    inner = mid0[2].reshape(48, 9, 48)
-    d02 = jnp.concatenate(
-        [
-            jnp.pad(taps, ((0, 0), (0, 0), (0, 80))),
-            jnp.pad(inner, ((0, 16), (0, 0), (64, 16))),
-        ]
-    ).reshape(256, 3, 384).transpose(1, 0, 2)
-    d12 = slotted(
-        jnp.concatenate([padded_rows(down_fin1[0, :192], 256), down_mid1[0, 0]]), 96, 128
-    )
-    fin03 = tapped(fin0[288:], 48)
-    fin13 = tapped(down_fin1[0, 192:], 96)
-    fin23 = down_fin2[0].T
-    place = jnp.stack([lax.axis_index("ty"), lax.axis_index("tx")]).astype(jnp.int32)
-
     vmem = pl.BlockSpec(memory_space=pltpu.VMEM)
     f32 = lambda *dims: pltpu.VMEM(dims, F32)
     bf = lambda *dims: pltpu.VMEM(dims, BF)
     outs = pl.pallas_call(
         main,
-        out_shape=[shape(64, 64, 48), shape(32, 32, 96), shape(16, 16, 192), shape(8, 8, 384)],
-        in_specs=[pl.BlockSpec(memory_space=pltpu.SMEM)] + [vmem] * 25,
+        out_shape=[shape(48, 64, 64), shape(32, 32, 96), shape(16, 16, 192), shape(8, 8, 384)],
+        in_specs=[vmem] * 14 + [pl.BlockSpec(memory_space=pltpu.HBM)] * 10,
         scratch_shapes=[
-            f32(6416, 48), f32(6320, 48), f32(6064, 48), bf(6400, 256), bf(2, 38 * 48, 192),
-            f32(1728, 128), f32(1840, 128), bf(2, 19 * 32, 384), f32(2, 544, 128), f32(600, 48),
-            f32(2080, 128), f32(2032, 128), f32(1840, 128), bf(2048, 384), bf(2, 19 * 32, 384),
-            f32(2, 544, 128), f32(600, 96),
-            f32(2, 768, 128), f32(2, 768, 128), f32(2, 704, 128), bf(768, 768),
-            f32(3, 224, 128), f32(3, 224, 128), f32(3, 176, 128), bf(208, 1152),
-            f32(1024, 48), f32(256, 48), f32(256, 96), f32(1024, 96), f32(256, 128), f32(64, 48),
+            bf(2, 96, 864), bf(2, 192, 1728), bf(2, 384, 3456), bf(3, 48, 432), bf(96, 864),
+            bf(672, 432), bf(576, 864), bf(1728, 384), bf(336, 384), bf(144, 192),
+            f32(6016, 48), f32(5856, 48), f32(5824, 48), bf(6000, 144), bf(2, 36 * 48, 144),
+            bf(256, 432), f32(1728, 128), f32(1760, 128), bf(2, 18 * 32, 144), bf(2, 18 * 32, 144),
+            f32(2, 544, 128), f32(544, 48), bf(64, 432),
+            f32(1888, 96), f32(1792, 96), f32(1760, 96), bf(1872, 288), bf(2, 18 * 32, 288),
+            f32(2, 544, 128), f32(544, 96), bf(64, 864),
+            f32(2, 688, 128), f32(2, 624, 128), f32(2, 576, 128), bf(672, 576), bf(64, 1728),
+            f32(3, 208, 128), f32(3, 176, 128), f32(3, 128, 128), bf(192, 1152),
+            f32(1024, 48), f32(256, 48), f32(256, 96), f32(1024, 96), f32(256, 128),
+            bf(1024, 96), f32(4, 64, 48), f32(3072, 64),
+            pltpu.SemaphoreType.DMA((10,)),
         ],
-        compiler_params=PARAMS,
+        compiler_params=MAIN_PARAMS,
     )(
-        place, *maps, above, below, cl, cr,
-        w0, w1, w2, block_w3, block_b0, block_b1, block_b2, block_b3,
-        up_w1[0], up_w2[0], up_w3[0], d01, d02, d12, fin03, fin13, fin23,
+        *maps, above, below, cl, cr,
+        block_w0, block_b0, block_b1, block_b2, block_b3, up_w1[0],
+        block_w1, block_w2, block_w3, down_mid0[0], down_mid1[0, 0],
+        down_fin0[0], down_fin1[0], down_fin2[0].T, up_w3[0], up_w2[0],
     )
-    return tuple(o.transpose(2, 0, 1) for o in outs)
+    return (outs[0],) + tuple(o.transpose(2, 0, 1) for o in outs[1:])
 
 
 def solution(mesh):

time: 99 us -> 57.1 us (0.58)
  Pallas kernels: 56.6 us -> 34.7 us
  local copies, waits for them, and re-layouts: 25.3 us -> 3.87 us
  waiting for transfers between devices: 1.62 us -> 7.32 us
  other arithmetic: 3.87 us -> 0 us
    pallas_call x1, Pallas kernels: 51.8 us -> 34.1 us  [per_device(): pl.pallas_call(main, out_shape=[shape(48, 64, 64), shape(32, 32, 96), sha...]
    unnamed x40 -> x20, local copies, waits for them, and re-layouts: 12.4 us -> 3.87 us
    ppermute x4, waiting for transfers between devices: 1.62 us -> 7.32 us  [ring(): return lax.ppermute(x, axis, [(i, (i + by) % n) for i in range(n)])]
    reshape x4 -> x0, local copies, waits for them, and re-layouts: 5.35 us -> none  [the longest x2 3.05 us: slotted(): return taps.reshape(3, w.shape[0], 3 * slot)]
    slice x13 -> x0, local copies, waits for them, and re-layouts: 4.45 us -> none  [the longest x1 1.8 us: per_device(): w1 = jnp.stack([slotted(block_w1[i], 96, 128) for i in range(2)])]
    another operation x4 -> x0, other arithmetic: 3.57 us -> none  [the longest x1 1.42 us: per_device(): jnp.stack([slotted(block_w2[i], 192, 256)[:, :, :704] for i in range(2)])]
    another operation x9 -> x0, local copies, waits for them, and re-layouts: 2.28 us -> none  [the longest x1 1.28 us: tapped(): return w.reshape(w.shape[0], 9, chan).transpose(1, 0, 2)]
    pallas_call x1, Pallas kernels: 2.6 us -> 0.43 us  [per_device(): pl.pallas_call(pack_cols, out_shape=[shape(RIGHT_ROWS, 128), shape(LEFT_R...]
  transfers between devices with their start and end apart: 4 -> 4, of which waited for: 1 -> 4; matrix products, arithmetic and copies ran while one was open for 23% -> 2% of each run, Pallas kernels for 0% -> 0%
where the time goes in v1:
time: 57.1 us; the launch traced here: 57 us
  Pallas kernels  34.7 us (61%)
  starting transfers between devices  10.2 us (18%)
  waiting for transfers between devices  7.32 us (13%)
  local copies, waits for them, and re-layouts  3.87 us (7%)
  between operations  0.89 us (2%)
    pallas_call x1, Pallas kernels, per_device(): pl.pallas_call(main, out_shape=[shape(48, 64, 64), shape(32, 32, 96), sha...  34.1 us
    ppermute x4, starting transfers between devices, ring(): return lax.ppermute(x, axis, [(i, (i + by) % n) for i in range(n)])  10.2 us
    ppermute x4, waiting for transfers between devices, ring(): return lax.ppermute(x, axis, [(i, (i + by) % n) for i in range(n)])  7.32 us
    unnamed x20, local copies, waits for them, and re-layouts  3.87 us
  transfers between devices with their start and end apart: 4, of which 4 were waited for; matrix products, arithmetic and copies ran while one was open for 2% of the time, Pallas kernels for 0%

profile of v1, /device:TPU:4, one launch (start us, length us, event | category | flops | bytes accessed | tf_op | source)
XLA Modules:
  0.0 57.0 jit_solution(8405015480264291431)
XLA Ops:
  0.6 0.0 copy-start.4
  0.6 0.0 copy-start.2
  0.7 0.0 copy-start.1
  0.7 2.0 %copy.24 = bf16[48,64,64]{0,2,1:T(8,128)(2,1)S(1)} copy(bf16[48,64,64]{2,1,0:T(8,128)(2,1)} %param.20) | data formatting | bytes 786432 | tf_op args[0]
  2.7 0.0 copy-start
  2.7 0.0 copy-done.4
  2.7 0.0 copy-done.2
  2.7 0.0 copy-done.1
  2.7 0.0 copy-start.6
  2.7 0.1 shard_map.219
  2.8 1.6 %collective-permute-start = (bf16[592,128]{1,0:T(8,128)(2,1)S(1)}, bf16[592,128]{1,0:T(8,128)(2,1)S(1)}, u32[]{:S(2)}, u32[]{:S(2)}) collective-permute-start(bf16[592,128]{1,0:T(8,128)(2,1)S(1)} %get-tuple-element.12), channel_id=1, source_target_pairs={{0,8},{8,16},{16,24},{24,32},{32,40},{40,48},{48,56},{56,0},{1,9},... | collective-permute-start | bytes 454664 | tf_op jit(solution)/shard_map/ppermute | solution.py:417
  4.5 2.6 %collective-permute-start.1 = (bf16[240,128]{1,0:T(8,128)(2,1)S(1)}, bf16[240,128]{1,0:T(8,128)(2,1)S(1)}, u32[]{:S(2)}, u32[]{:S(2)}) collective-permute-start(bf16[240,128]{1,0:T(8,128)(2,1)S(1)} %get-tuple-element.13), channel_id=1, source_target_pairs={{0,56},{8,0},{16,8},{24,16},{32,24},{40,32},{48,40},{56,48},{1,57}... | collective-permute-start | bytes 184328 | tf_op jit(solution)/shard_map/ppermute | solution.py:417
  7.0 1.9 %collective-permute-done.1.below = bf16[240,128]{1,0:T(8,128)(2,1)S(1)} collective-permute-done((bf16[240,128]{1,0:T(8,128)(2,1)S(1)}, bf16[240,128]{1,0:T(8,128)(2,1)S(1)}, u32[]{:S(2)}, u32[]{:S(2)}) %collective-permute-start.1) | collective-permute-done | bytes 61472 | tf_op jit(solution)/shard_map/ppermute | solution.py:417
  8.9 0.0 copy-start.5
  8.9 1.8 %collective-permute-done.above = bf16[592,128]{1,0:T(8,128)(2,1)S(1)} collective-permute-done((bf16[592,128]{1,0:T(8,128)(2,1)S(1)}, bf16[592,128]{1,0:T(8,128)(2,1)S(1)}, u32[]{:S(2)}, u32[]{:S(2)}) %collective-permute-start) | collective-permute-done | bytes 151584 | tf_op jit(solution)/shard_map/ppermute | solution.py:417
  10.7 0.0 copy-start.3
  10.7 0.4 shard_map.220
  11.1 0.0 copy-done
  11.1 2.0 %collective-permute-start.2 = (bf16[928,128]{1,0:T(8,128)(2,1)S(1)}, bf16[928,128]{1,0:T(8,128)(2,1)S(1)}, u32[]{:S(2)}, u32[]{:S(2)}) collective-permute-start(bf16[928,128]{1,0:T(8,128)(2,1)S(1)} %get-tuple-element.14), channel_id=1, source_target_pairs={{0,1},{1,2},{2,3},{3,4},{4,5},{5,6},{6,7},{7,0},{8,9},{9,10},{10,1... | collective-permute-start | bytes 712712 | tf_op jit(solution)/shard_map/ppermute | solution.py:417
  13.1 4.0 %collective-permute-start.3 = (bf16[400,128]{1,0:T(8,128)(2,1)S(1)}, bf16[400,128]{1,0:T(8,128)(2,1)S(1)}, u32[]{:S(2)}, u32[]{:S(2)}) collective-permute-start(bf16[400,128]{1,0:T(8,128)(2,1)S(1)} %get-tuple-element.15), channel_id=1, source_target_pairs={{0,7},{1,0},{2,1},{3,2},{4,3},{5,4},{6,5},{7,6},{8,15},{9,8},{10,9... | collective-permute-start | bytes 307208 | tf_op jit(solution)/shard_map/ppermute | solution.py:417
  17.2 0.0 copy-done.6
  17.2 1.1 %copy.25 = bf16[1,672,432]{2,1,0:T(8,128)(2,1)} copy(bf16[1,672,432]{1,2,0:T(8,128)(2,1)S(1)} %copy-done.6) | data formatting | bytes 1161216 | tf_op args[17]
  18.3 0.0 copy-done.5
  18.3 0.0 copy-done.3
  18.3 1.1 %collective-permute-done.3.cr = bf16[400,128]{1,0:T(8,128)(2,1)S(1)} collective-permute-done((bf16[400,128]{1,0:T(8,128)(2,1)S(1)}, bf16[400,128]{1,0:T(8,128)(2,1)S(1)}, u32[]{:S(2)}, u32[]{:S(2)}) %collective-permute-start.3) | collective-permute-done | bytes 102432 | tf_op jit(solution)/shard_map/ppermute | solution.py:417
  19.4 0.0 copy-start.8
  19.4 2.6 %collective-permute-done.2.cl = bf16[928,128]{1,0:T(8,128)(2,1)S(1)} collective-permute-done((bf16[928,128]{1,0:T(8,128)(2,1)S(1)}, bf16[928,128]{1,0:T(8,128)(2,1)S(1)}, u32[]{:S(2)}, u32[]{:S(2)}) %collective-permute-start.2) | collective-permute-done | bytes 237600 | tf_op jit(solution)/shard_map/ppermute | solution.py:417
  22.0 0.0 copy-start.7
  22.0 0.0 copy-done.8
  22.0 0.7 %copy-done.7 = bf16[928,128]{1,0:T(8,128)(2,1)} copy-done((bf16[928,128]{1,0:T(8,128)(2,1)}, bf16[928,128]{1,0:T(8,128)(2,1)S(1)}, u32[]{:S(2)}) %copy-start.7) | copy-done | bytes 237592
  22.7 34.1 %shard_map.221 = (bf16[48,64,64]{2,1,0:T(8,128)(2,1)}, bf16[32,32,96]{2,1,0:T(8,128)(2,1)}, bf16[16,16,192]{2,1,0:T(8,128)(2,1)}, bf16[8,8,384]{2,1,0:T(8,128)(2,1)}) custom-call(bf16[64,64,48]{2,1,0:T(8,128)(2,1)} %bitcast.19, bf16[32,32,96]{2,1,0:T(8,128)(2,1)} %bitcast.20, bf16[16,16,192]{2,1,0:T(8,128)(2,1)} %bitcast.23, bf16[8,8,384]{2,1,0:T(8,128)(2,1)} %bitcast.26, ...), custom_call_target="tpu_custom_call" | custom-call | tf_op jit(solution)/shard_map/pallas_call | solution.py:449
Async XLA Ops:
  0.6 2.0 %copy-start.4 = (bf16[384,8,8]{0,2,1:T(8,128)(2,1)S(1)}, bf16[384,8,8]{0,2,1:T(8,128)(2,1)}, u32[]{:S(2)}) copy-start(bf16[384,8,8]{0,2,1:T(8,128)(2,1)} %param.23) | copy-start | bytes 147460
  0.6 2.0 %copy-start.2 = (bf16[192,16,16]{0,2,1:T(8,128)(2,1)S(1)}, bf16[192,16,16]{0,2,1:T(8,128)(2,1)}, u32[]{:S(2)}) copy-start(bf16[192,16,16]{0,2,1:T(8,128)(2,1)} %param.22) | copy-start | bytes 294916
  0.7 2.0 %copy-start.1 = (bf16[96,32,32]{0,2,1:T(8,128)(2,1)S(1)}, bf16[96,32,32]{0,2,1:T(8,128)(2,1)}, u32[]{:S(2)}) copy-start(bf16[96,32,32]{0,2,1:T(8,128)(2,1)} %param.21) | copy-start | bytes 589828
  2.7 8.5 %copy-start = (bf16[48,64,64]{0,2,1:T(8,128)(2,1)}, bf16[48,64,64]{0,2,1:T(8,128)(2,1)S(1)}, u32[]{:S(2)}) copy-start(bf16[48,64,64]{0,2,1:T(8,128)(2,1)S(1)} %copy.24) | copy-start | bytes 1179652
  2.7 14.5 %copy-start.6 = (bf16[1,672,432]{1,2,0:T(8,128)(2,1)S(1)}, bf16[1,672,432]{1,2,0:T(8,128)(2,1)}, u32[]{:S(2)}) copy-start(bf16[1,672,432]{1,2,0:T(8,128)(2,1)} %param.37) | copy-start | bytes 1741828
  2.8 7.9 %collective-permute-start = (bf16[592,128]{1,0:T(8,128)(2,1)S(1)}, bf16[592,128]{1,0:T(8,128)(2,1)S(1)}, u32[]{:S(2)}, u32[]{:S(2)}) collective-permute-start(bf16[592,128]{1,0:T(8,128)(2,1)S(1)} %get-tuple-element.12), channel_id=1, source_target_pairs={{0,8},{8,16},{16,24},{24,32},{32,40},{40,48},{48,56},{56,0},{1,9},... | collective-permute-start | bytes 454664 | tf_op jit(solution)/shard_map/ppermute | solution.py:417
  4.5 4.4 %collective-permute-start.1 = (bf16[240,128]{1,0:T(8,128)(2,1)S(1)}, bf16[240,128]{1,0:T(8,128)(2,1)S(1)}, u32[]{:S(2)}, u32[]{:S(2)}) collective-permute-start(bf16[240,128]{1,0:T(8,128)(2,1)S(1)} %get-tuple-element.13), channel_id=1, source_target_pairs={{0,56},{8,0},{16,8},{24,16},{32,24},{40,32},{48,40},{56,48},{1,57}... | collective-permute-start | bytes 184328 | tf_op jit(solution)/shard_map/ppermute | solution.py:417
  8.9 9.4 %copy-start.5 = (bf16[240,128]{1,0:T(8,128)(2,1)}, bf16[240,128]{1,0:T(8,128)(2,1)S(1)}, u32[]{:S(2)}) copy-start(bf16[240,128]{1,0:T(8,128)(2,1)S(1)} %collective-permute-done.1.below) | copy-start | bytes 184324
  10.7 7.6 %copy-start.3 = (bf16[592,128]{1,0:T(8,128)(2,1)}, bf16[592,128]{1,0:T(8,128)(2,1)S(1)}, u32[]{:S(2)}) copy-start(bf16[592,128]{1,0:T(8,128)(2,1)S(1)} %collective-permute-done.above) | copy-start | bytes 454660
  11.1 10.8 %collective-permute-start.2 = (bf16[928,128]{1,0:T(8,128)(2,1)S(1)}, bf16[928,128]{1,0:T(8,128)(2,1)S(1)}, u32[]{:S(2)}, u32[]{:S(2)}) collective-permute-start(bf16[928,128]{1,0:T(8,128)(2,1)S(1)} %get-tuple-element.14), channel_id=1, source_target_pairs={{0,1},{1,2},{2,3},{3,4},{4,5},{5,6},{6,7},{7,0},{8,9},{9,10},{10,1... | collective-permute-start | bytes 712712 | tf_op jit(solution)/shard_map/ppermute | solution.py:417
  13.1 6.3 %collective-permute-start.3 = (bf16[400,128]{1,0:T(8,128)(2,1)S(1)}, bf16[400,128]{1,0:T(8,128)(2,1)S(1)}, u32[]{:S(2)}, u32[]{:S(2)}) collective-permute-start(bf16[400,128]{1,0:T(8,128)(2,1)S(1)} %get-tuple-element.15), channel_id=1, source_target_pairs={{0,7},{1,0},{2,1},{3,2},{4,3},{5,4},{6,5},{7,6},{8,15},{9,8},{10,9... | collective-permute-start | bytes 307208 | tf_op jit(solution)/shard_map/ppermute | solution.py:417
  19.4 2.6 %copy-start.8 = (bf16[400,128]{1,0:T(8,128)(2,1)}, bf16[400,128]{1,0:T(8,128)(2,1)S(1)}, u32[]{:S(2)}) copy-start(bf16[400,128]{1,0:T(8,128)(2,1)S(1)} %collective-permute-done.3.cr) | copy-start | bytes 307204
  22.0 0.7 %copy-start.7 = (bf16[928,128]{1,0:T(8,128)(2,1)}, bf16[928,128]{1,0:T(8,128)(2,1)S(1)}, u32[]{:S(2)}) copy-start(bf16[928,128]{1,0:T(8,128)(2,1)S(1)} %collective-permute-done.2.cl) | copy-start | bytes 712708

commit v2 on v1

v2 whole, which is shorter than its diff:
```python
import functools

import jax
import jax.numpy as jnp
from jax import lax
from jax.experimental import pallas as pl
from jax.experimental.pallas import tpu as pltpu
from jax.sharding import PartitionSpec as P

BF = jnp.bfloat16
F32 = jnp.float32
TILE = (64, 32, 16, 8)
CHAN = (48, 96, 192, 384)
LEAD = (9, 5, 3, 2)
EXT = (75, 39, 21, 12)
PITCH = (80, 48, 32, 16)
TALL = (80, 48, 32, 16)
GROUP = (16, 16, 16, 8)
DOWN_ROWS, UP_ROWS = 592, 240
RIGHT_ROWS, LEFT_ROWS = 928, 400
PARAMS = pltpu.CompilerParams(vmem_limit_bytes=16 * 2**20)
MAIN_PARAMS = pltpu.CompilerParams(vmem_limit_bytes=44 * 2**20)


def spans(chan):
    return [(lo, min(lo + 128, chan)) for lo in range(0, chan, 128)]


def put_packed(ref, at, value, branch, split):
    if branch == 0:
        ref[at : at + split, 0:48] = value[:split]
        ref[at : at + value.shape[0] - split, 64:112] = value[split:]
        return at + split
    for lo, hi in spans(CHAN[branch]):
        ref[at : at + value.shape[0], 0 : hi - lo] = value[:, lo:hi]
        at += value.shape[0]
    return at


def take_packed(ref, at, count, branch, split):
    if branch == 0:
        return jnp.concatenate(
            [ref[at : at + split, 0:48], ref[at : at + count - split, 64:112]], axis=0
        ), at + split
    parts = []
    for lo, hi in spans(CHAN[branch]):
        parts.append(ref[at : at + count, 0 : hi - lo])
        at += count
    return (parts[0] if len(parts) == 1 else jnp.concatenate(parts, axis=1)), at


def flat_rows(ref, lo, hi, branch):
    side = TILE[branch]
    value = ref[lo:hi].astype(F32)
    return value.reshape((hi - lo) * side, CHAN[branch]).astype(BF)


def pack_rows(f0, f1, f2, f3, down, up):
    at = 0
    for b, f in enumerate((f0, f1, f2, f3)):
        at = put_packed(down, at, flat_rows(f, TILE[b] - LEAD[b], TILE[b], b), b, 288)
    at = 0
    for b, f in enumerate((f0, f1, f2, f3)):
        at = put_packed(up, at, flat_rows(f, 0, 2, b), b, 64)


def pack_cols(f0, f1, f2, f3, above, below, right, left, work):
    down_at = up_at = right_at = left_at = 0
    for b, f in enumerate((f0, f1, f2, f3)):
        side, lead, chan, group = TILE[b], LEAD[b], CHAN[b], GROUP[b]
        high, down_at = take_packed(above, down_at, lead * side, b, 288)
        low, up_at = take_packed(below, up_at, 2 * side, b, 64)
        parts = (
            (high.astype(F32).reshape(lead, side, chan), 0, lead),
            (f[...].astype(F32).reshape(side, side, chan), lead, side),
            (low.astype(F32).reshape(2, side, chan), lead + side, 2),
        )
        for last in (True, False):
            cut = slice(side - group, side) if last else slice(0, group)
            for value, start, count in parts:
                edge = value[:, cut].reshape(count * group, chan)
                for s, (lo, hi) in enumerate(spans(chan)):
                    work[s, start * group : (start + count) * group, 0 : hi - lo] = edge[:, lo:hi]
            columns = range(group - lead, group) if last else range(2)
            cols = []
            for k in columns:
                planes = [
                    work[s, pl.ds(k, TALL[b], stride=group), 0 : hi - lo]
                    for s, (lo, hi) in enumerate(spans(chan))
                ]
                cols.append([p.astype(BF) for p in planes])
            target, at = (right, right_at) if last else (left, left_at)
            if b == 0:
                half = 5 if last else 1
                for i, (col,) in enumerate(cols):
                    place = at + (i if i < half else i - half) * TALL[0]
                    lane = 0 if i < half else 64
                    target[place : place + TALL[0], lane : lane + 48] = col
                at += half * TALL[0]
            else:
                for s, (lo, hi) in enumerate(spans(chan)):
                    for col in cols:
                        target[at : at + TALL[b], 0 : hi - lo] = col[s]
                        at += TALL[b]
            if last:
                right_at = at
            else:
                left_at = at


def clear_edges(place, planes, per, pitch, height, breadth, lead, trail):
    groups = -(-height // per)

    def rows(lo, count):
        for r in range(lo, lo + count):
            spot = slice(r // per * pitch, (r // per + 1) * pitch)
            if per == 4:
                lane = 64 * (r % 2)
                planes[r % 4 // 2][spot, lane : lane + 64] = jnp.zeros((pitch, 64), F32)
            else:
                for ref in [planes[r % 2]] if per == 2 else planes:
                    ref[spot, :] = jnp.zeros((pitch, ref.shape[1]), F32)

    def cols(lo, count):
        for ref in planes:
            for k in range(lo, lo + count):
                ref[pl.ds(k, groups, stride=pitch), :] = jnp.zeros((groups, ref.shape[1]), F32)

    if lead:
        pl.when(place[0] == 0)(lambda: rows(0, lead))
        pl.when(place[1] == 0)(lambda: cols(0, lead))
    if trail:
        pl.when(place[0] == 7)(lambda: rows(height - trail, trail))
        pl.when(place[1] == 7)(lambda: cols(breadth - trail, trail))


def prepare(w0, w1, b0, b1, mid0, mid1, fin0, fin1, q0, q1, c0, c1, d01, d02, d12):
    for out in (q0, q1, c0, c1):
        out[...] = jnp.zeros_like(out)
    for w, q, bias, c, chan, per, slot in ((w0, q0, b0, c0, 48, 4, 64), (w1, q1, b1, c1, 96, 2, 128)):
        for j in range(per):
            c[:, j * slot : j * slot + chan] = bias[...]
            for dy in range(3):
                more, r = divmod(j + dy, per)
                for dx in range(3):
                    lane = more * 768 + dx * 256 + r * slot
                    tap = (dy * 3 + dx) * chan
                    for i in range(2):
                        q[i, j * slot : j * slot + chan, lane : lane + chan] = w[i, :, tap : tap + chan]


    for out in (d01, d02, d12):
        out[...] = jnp.zeros_like(out)
    for tap in range(9):
        dy, dx = divmod(tap, 3)
        cut = slice(tap * 48, tap * 48 + 48)
        lane = dy // 2 * 384 + dx * 128 + dy % 2 * 64
        d01[0:96, lane : lane + 48] = fin0[0:96, cut]
        d01[128:176, lane : lane + 48] = mid0[0, :, cut]
        d01[192:240, lane : lane + 48] = mid0[1, :, cut]
        lane = dy * 384 + dx * 128
        d02[0:192, lane : lane + 48] = fin0[96:288, cut]
        d02[192:240, lane + 64 : lane + 112] = mid0[2, :, cut]
        cut = slice(tap * 96, tap * 96 + 96)
        d12[0:192, lane : lane + 96] = fin1[0:192, cut]
        d12[256:352, lane : lane + 96] = mid1[:, cut]


def dot_nt(x, w):
    return lax.dot_general(x, w, (((1,), (1,)), ((), ())), preferred_element_type=F32)


def rounded(x):
    return x.astype(BF).astype(F32)


PER = (4, 2, 1, 1)


def main(f0, f1, f2, f3, above, below, cl, cr, b0, b1, b2, b3, u1, *rest):
    ready, far, rest = rest[:5], rest[5:12], rest[12:]
    outs, near, scratch = rest[:4], rest[4:11], rest[11:-1]
    main_body(
        f0, f1, f2, f3, above, below, cl, cr, b0, b1, b2, b3, u1, ready, far, near, rest[-1], *outs, *scratch
    )


def main_body(
    f0, f1, f2, f3, above, below, cl, cr, b0, b1, b2, b3, u1, ready, far, near, sems,
    j0, j1, j2, j3,
    x0, h0, a0, s0, t0, v01, v0, ta, vv02, n03, g03,
    x1, h1, a1, s1, t1, vv12, m13, g13,
    x2, h2, a2, s2, g23,
    x3, h3, a3, s3,
    z1, z2, y2, y1, wide, c1, mcol, jt, col_in, col_out, zw,
):
    copies = [pltpu.make_async_copy(a, b, sems.at[i]) for i, (a, b) in enumerate(zip(far, near))]
    for copy in copies:
        copy.start()
    q0, q1, d01, d02, d12 = ready
    w2, w3, fin0, fin1, fin2, u3, u2 = near
    place = (lax.axis_index("ty"), lax.axis_index("tx"))
    feats = (f0, f1, f2, f3)
    two = lambda ref: [ref.at[0], ref.at[1]]
    three = lambda ref: [ref.at[i] for i in range(3)]
    xs = (two(x0), two(x1), two(x2), three(x3))
    hs = (two(h0), two(h1), two(h2), three(h3))
    as_ = (two(a0), two(a1), two(a2), three(a3))
    x0[...] = jnp.zeros_like(x0)
    x1[...] = jnp.zeros_like(x1)

    def put_row(b, r, row):
        side, lead, pitch = TILE[b], LEAD[b], PITCH[b]
        spot = pl.ds(r // PER[b] * pitch + lead, side)
        if b == 0:
            lane = 64 * (r % 2)
            x0[r % 4 // 2, spot, lane : lane + 48] = row
        elif b == 1:
            x1[r % 2, spot, 0:96] = row
        else:
            for s, (lo, hi) in enumerate(spans(CHAN[b])):
                xs[b][s][spot, 0 : hi - lo] = row[:, lo:hi]

    def assemble(b, ats):
        side, lead, chan, pitch = TILE[b], LEAD[b], CHAN[b], PITCH[b]
        down_at, up_at, right_at, left_at = ats
        high, down_at = take_packed(above, down_at, lead * side, b, 288)
        low, up_at = take_packed(below, up_at, 2 * side, b, 64)
        for value, start, count in ((high, 0, lead), (low, lead + side, 2)):
            for y in range(count):
                put_row(b, start + y, value[y * side : (y + 1) * side].astype(F32))
        for y in range(side):
            put_row(b, lead + y, feats[b][y].astype(F32))
        for ref, at, count, begin, half in ((cl, right_at, lead, 0, 5), (cr, left_at, 2, lead + side, 1)):
            if b == 0:
                for i in range(count):
                    spot = at + (i if i < half else i - half) * TALL[0]
                    lane = 0 if i < half else 64
                    col_in[...] = ref[spot : spot + TALL[0], lane : lane + 48].astype(F32)
                    for j in range(4):
                        n = (EXT[0] - j + 3) // 4
                        lane = 64 * (j % 2)
                        col_out[i % 2, j // 2, 0:n, lane : lane + 48] = col_in[pl.ds(j, n, stride=4), :]
                    for s in range(2):
                        x0[s, pl.ds(begin + i, 19, stride=pitch), :] = col_out[i % 2, s, 0:19, :]
                at += half * TALL[0]
            else:
                for s, (lo, hi) in enumerate(spans(chan)):
                    for i in range(count):
                        col = ref[at : at + TALL[b], 0 : hi - lo].astype(F32)
                        at += TALL[b]
                        if b == 1:
                            col_out[0, 0, 0 : TALL[1], 0:96] = col
                            for j in range(2):
                                n = (EXT[1] - j + 1) // 2
                                x1[j, pl.ds(begin + i, n, stride=pitch), :] = col_out[0, 0, pl.ds(j, n, stride=2), :]
                        else:
                            xs[b][s][pl.ds(begin + i, EXT[b], stride=pitch), 0 : hi - lo] = col[: EXT[b]]
            if ref is cl:
                right_at = at
            else:
                left_at = at
        clear_edges(place, xs[b], PER[b], pitch, EXT[b], EXT[b], lead, 2)
        return down_at, up_at, right_at, left_at

    col_out[...] = jnp.zeros_like(col_out)
    ats = (0, 0, 0, 0)
    for b in range(4):
        ats = assemble(b, ats)

    def steps(rows, count, body):
        step = rows // count
        if count == 1:
            body(0, step)
            return

        @pl.loop(0, count)
        def _(i):
            body(pl.multiple_of(i * step, 16), step)

    def spread(planes, target, rows, count, slot):
        def body(p, step):
            for dx in range(3):
                for s, plane in enumerate(planes):
                    piece = plane[pl.ds(p + dx, step), :].astype(BF)
                    target[pl.ds(p, step), dx * slot + s * 128 : dx * slot + s * 128 + 128] = piece

        steps(rows, count, body)

    def side_by_side(planes, target, rows):
        for tap in range(9):
            at = tap // 3 * 32 + tap % 3
            piece = jnp.concatenate(
                [planes[0][at : at + rows, :], planes[1][at : at + rows, 0:64]], axis=1
            )
            target[0:rows, tap * 192 : tap * 192 + 192] = piece.astype(BF)

    def block(b, weight, bias, source, counts):
        pitch, chan, lead, per = PITCH[b], CHAN[b], LEAD[b], PER[b]
        reach = (2, 2, 1, 3)[b]
        slot = 384 if b == 3 else 256

        def conv(i, p, step):
            taps = [source[pl.ds(p + k * pitch, step), :] for k in range(reach)]
            return dot_nt(jnp.concatenate(taps, axis=1), weight[i]) + bias[i : i + 1, :]

        def cuts(total):
            return [(s, lo, hi) for s, (lo, hi) in enumerate(spans(total.shape[1]))]

        def inner(p, step):
            value = jnp.maximum(conv(0, p, step), 0.0)
            for s, lo, hi in cuts(value):
                hs[b][s][pl.ds(p, step), 0 : hi - lo] = value[:, lo:hi]

        def outer(p, step):
            total = conv(1, p, step)
            for s, lo, hi in cuts(total):
                if per == 4:
                    kept = x0[1 - s, pl.ds(p + s * pitch + 2, step), :]
                elif per == 2:
                    kept = x1[s, pl.ds(p + pitch + 2, step), :]
                else:
                    kept = xs[b][s][pl.ds(p + 2 * pitch + 2, step), 0 : hi - lo]
                value = rounded(jnp.maximum(kept + total[:, lo:hi], 0.0))
                as_[b][s][pl.ds(p, step), 0 : hi - lo] = value

        inner_rows = -(-(EXT[b] - 2) // per) * pitch
        outer_rows = -(-(EXT[b] - 4) // per) * pitch
        extra = (reach - 1) * pitch
        if b == 2:
            side_by_side(xs[b], source, inner_rows)
        else:
            spread(xs[b], source, inner_rows + extra, counts[0], slot)
        steps(inner_rows, counts[1], inner)
        clear_edges(place, hs[b], per, pitch, EXT[b] - 2, EXT[b] - 2, lead - 1, 1)
        if b == 2:
            side_by_side(hs[b], source, outer_rows)
        else:
            spread(hs[b], source, outer_rows + extra, counts[2], slot)
        steps(outer_rows, counts[3], outer)
        clear_edges(place, as_[b], per, pitch, EXT[b] - 4, EXT[b] - 4, lead - 2, 0)

    block(0, q0, b0, s0, (5, 5, 5, 5))
    block(1, q1, b1, s1, (3, 3, 3, 3))
    copies[0].wait()
    block(2, w2, b2, s2, (1, 2, 1, 2))
    copies[1].wait()
    block(3, w3, b3, s3, (1, 1, 1, 1))
    for copy in copies[2:]:
        copy.wait()

    for pair in range(36):
        for dx in range(3):
            piece = a0[pair % 2, pl.ds(pair // 2 * 80 + dx, 48, stride=2), :]
            t0[pair * 48 : pair * 48 + 48, dx * 128 : dx * 128 + 128] = piece.astype(BF)

    def first(p, step):
        both = jnp.concatenate([t0[pl.ds(p, step), :], t0[pl.ds(p + 48, step), :]], axis=1)
        total = dot_nt(both, d01[...])
        v01[pl.ds(p, step), :] = rounded(total[:, :128])
        v0[pl.ds(p, step), :] = rounded(jnp.maximum(total[:, 128:], 0.0))

    steps(35 * 48, 5, first)
    clear_edges(place, [v0], 1, 48, 35, 35, 3, 0)

    for row in range(35):
        spot = slice(row // 2 * 32, row // 2 * 32 + 32)
        for dx in range(3):
            lane = slice(dx * 128, dx * 128 + 128)
            ta[row % 2, spot, lane] = v0[pl.ds(row * 48 + dx, 32, stride=2), :].astype(BF)
            piece = a1[row % 2, pl.ds(row // 2 * 48 + dx, 32, stride=2), :]
            t1[row % 2, spot, lane] = piece.astype(BF)

    def second(source, p, n, weight):
        taps = [source[dy % 2, p + dy // 2 * 32 : p + dy // 2 * 32 + n, :] for dy in range(3)]
        return dot_nt(jnp.concatenate(taps, axis=1), weight[...])

    for p, n in ((0, 272), (272, 272)):
        cut = slice(p, p + n)
        total = second(ta, p, n, d02)
        vv02[0, cut, :] = rounded(total[:, :128])
        vv02[1, cut, 0:64] = rounded(total[:, 128:192])
        n03[cut, :] = rounded(jnp.maximum(total[:, 192:240], 0.0))
        total = second(t1, p, n, d12)
        vv12[0, cut, :] = rounded(total[:, :128])
        vv12[1, cut, 0:64] = rounded(total[:, 128:192])
        m13[cut, :] = rounded(jnp.maximum(total[:, 256:352], 0.0))

    clear_edges(place, [n03], 1, 32, 17, 17, 1, 0)
    clear_edges(place, [m13], 1, 32, 17, 17, 1, 0)

    def gathered(ref, width, dy, dx):
        return jnp.concatenate(
            [ref[pl.ds((2 * i + dy) * 32 + dx, 8, stride=2), 0:width] for i in range(8)], axis=0
        ).astype(BF)

    for tap in range(9):
        dy, dx = divmod(tap, 3)
        g03[:, tap * 48 : tap * 48 + 48] = gathered(n03, 48, dy, dx)
        g13[:, tap * 96 : tap * 96 + 96] = gathered(m13, 96, dy, dx)
        for s, (lo, hi) in enumerate(spans(192)):
            g23[:, tap * 192 + lo : tap * 192 + hi] = gathered(a2.at[s], hi - lo, dy, dx)
    t03 = dot_nt(g03[...], fin0[288:672, :])
    t13 = dot_nt(g13[...], fin1[192:576, :])
    t23 = jnp.dot(g23[...], fin2[...], preferred_element_type=F32)

    c3 = [
        jnp.concatenate([a3[s, y * 16 : y * 16 + 8, :] for y in range(8)], axis=0) for s in range(3)
    ]
    c3 = jnp.concatenate(c3, axis=1)
    three = jnp.maximum(c3 + rounded(t03) + rounded(t13) + rounded(t23), 0.0)
    j3[...] = three.reshape(8, 8, 384).astype(BF)

    c3b = c3.astype(BF)
    t30 = rounded(dot_nt(c3b, u3[0:48, :]))
    t31 = rounded(dot_nt(c3b, u3[48:144, :]))
    t32 = rounded(dot_nt(c3b, u3[144:336, :]))
    c2 = [
        jnp.concatenate([a2[s, pl.ds((y + 1) * 32 + 1, 16), 0 : hi - lo] for y in range(16)], axis=0)
        for s, (lo, hi) in enumerate(spans(192))
    ]
    c2 = jnp.concatenate(c2, axis=1)
    c2b = c2.astype(BF)
    t20 = rounded(dot_nt(c2b, u2[0:48, :]))
    t21 = rounded(dot_nt(c2b, u2[48:144, :]))

    def doubled(target, small, side, lanes):
        for y in range(side):
            row = small[y * side : (y + 1) * side]
            for odd in range(2):
                for right in range(2):
                    target[pl.ds((2 * y + odd) * 2 * side + right, side, stride=2), 0:lanes] = row

    for s, (lo, hi) in enumerate(spans(192)):
        doubled(wide, t32[:, lo:hi], 8, hi - lo)
        for y in range(16):
            t02 = vv02[s, pl.ds((y + 1) * 32 + 1, 16), 0 : hi - lo]
            t12 = vv12[s, pl.ds((y + 1) * 32 + 1, 16), 0 : hi - lo]
            keep = c2[y * 16 : (y + 1) * 16, lo:hi]
            row = keep + t02 + t12 + wide[pl.ds(y * 16, 16), 0 : hi - lo]
            j2[y, :, lo:hi] = jnp.maximum(row, 0.0).astype(BF)

    doubled(z2, t30, 8, 48)
    sum2 = z2[...] + t20
    doubled(z1, sum2, 16, 48)
    doubled(y2, t31, 8, 96)
    sum2 = y2[...] + t21
    doubled(y1, sum2, 16, 96)

    for y in range(32):
        row = a1[(y + 3) % 2, pl.ds((y + 3) // 2 * 48 + 3, 32), 0:96]
        c1[y * 32 : y * 32 + 32, :] = row.astype(BF)
    total = z1[...] + rounded(dot_nt(c1[...], u1[...]))
    zw[32:1056, 0:48] = total
    zw[0:1024, 64:112] = total

    def last_rows(m, plane, group, k):
        for right in range(2):
            mcol[k, pl.ds(right, 32, stride=2), :] = zw[pl.ds(m * 32, 32), :]
        zero = a0[plane, pl.ds(group * 80 + 7, 64), :]
        turned = jnp.maximum(zero + mcol[k], 0.0).T
        jt[pl.ds(2 * m + 7, 48, stride=80), :] = turned[0:48]
        jt[pl.ds(2 * m + 8, 48, stride=80), :] = turned[64:112]

    @pl.loop(0, 8)
    def _(i):
        for k in range(4):
            y = 4 * i + k
            spot = pl.ds(pl.multiple_of(y * 32, 32), 32)
            one = a1[(k + 3) % 2, pl.ds((2 * i + (k + 3) // 2) * 48 + 3, 32), 0:96]
            t01 = v01[pl.ds((y + 3) * 48 + 3, 32), 0:96]
            j1[y] = jnp.maximum(one + t01 + y1[spot, :], 0.0).astype(BF)
            last_rows(y, (3 + k) % 2, 2 * i + (3 + k) // 2, k)

    last_rows(32, 1, 17, 0)

    @pl.loop(0, 6)
    def _(i):
        for c in range(8):
            c = 8 * i + c
            j0[c] = jt[pl.ds(pl.multiple_of(c * 80 + 8, 8), 64), :].astype(BF)


def ring(x, axis, by):
    n = lax.axis_size(axis)
    return lax.ppermute(x, axis, [(i, (i + by) % n) for i in range(n)])


def shape(*dims, kind=BF):
    return jax.ShapeDtypeStruct(dims, kind)


def per_device(
    feat0, feat1, feat2, feat3,
    block_w0, block_w1, block_w2, block_w3,
    block_b0, block_b1, block_b2, block_b3,
    up_w1, up_w2, up_w3,
    down_mid0, down_mid1, down_fin0, down_fin1, down_fin2,
):
    maps = [f.transpose(1, 2, 0) for f in (feat0, feat1, feat2, feat3)]
    down, up = pl.pallas_call(
        pack_rows,
        out_shape=[shape(DOWN_ROWS, 128), shape(UP_ROWS, 128)],
        compiler_params=PARAMS,
    )(*maps)
    above, below = ring(down, "ty", 1), ring(up, "ty", -1)
    fin0, fin1, mid0, mid1 = down_fin0[0], down_fin1[0], down_mid0[0], down_mid1[0, 0]
    above, below, fin0 = lax.optimization_barrier((above, below, fin0))
    right, left = pl.pallas_call(
        pack_cols,
        out_shape=[shape(RIGHT_ROWS, 128), shape(LEFT_ROWS, 128)],
        scratch_shapes=[pltpu.VMEM((3, 80 * 16, 128), F32)],
        compiler_params=PARAMS,
    )(*maps, above, below)
    cl, cr = ring(right, "tx", 1), ring(left, "tx", -1)

    q0, q1, c0, c1, d01, d02, d12 = pl.pallas_call(
        prepare,
        out_shape=[
            shape(2, 256, 1536), shape(2, 256, 1536), shape(2, 256, kind=F32), shape(2, 256, kind=F32),
            shape(256, 768), shape(256, 1152), shape(352, 1152),
        ],
        compiler_params=PARAMS,
    )(block_w0, block_w1, block_b0, block_b1, mid0, mid1, fin0, fin1)

    vmem = pl.BlockSpec(memory_space=pltpu.VMEM)
    f32 = lambda *dims: pltpu.VMEM(dims, F32)
    bf = lambda *dims: pltpu.VMEM(dims, BF)
    ready = (q0, q1, d01, d02, d12)
    far = (block_w2, block_w3, fin0, fin1, down_fin2[0].T, up_w3[0], up_w2[0])
    outs = pl.pallas_call(
        main,
        out_shape=[shape(48, 64, 64), shape(32, 32, 96), shape(16, 16, 192), shape(8, 8, 384)],
        in_specs=[vmem] * 18 + [pl.BlockSpec(memory_space=pltpu.HBM)] * 7,
        scratch_shapes=[bf(*w.shape) for w in far]
        + [
            f32(2, 1616, 128), f32(2, 1536, 128), f32(2, 1536, 128), bf(1600, 768), bf(1728, 384),
            f32(1728, 128), f32(1760, 128), bf(2, 18 * 32, 384), f32(2, 544, 128), f32(544, 48), bf(64, 432),
            f32(2, 976, 128), f32(2, 928, 128), f32(2, 896, 128), bf(960, 768), bf(2, 18 * 32, 384),
            f32(2, 544, 128), f32(544, 96), bf(64, 864),
            f32(2, 688, 128), f32(2, 624, 128), f32(2, 576, 128), bf(608, 1728), bf(64, 1728),
            f32(3, 208, 128), f32(3, 176, 128), f32(3, 128, 128), bf(192, 1152),
            f32(1024, 48), f32(256, 48), f32(256, 96), f32(1024, 96), f32(256, 128),
            bf(1024, 96), f32(4, 64, 128), f32(3840, 64), f32(80, 48), f32(2, 2, 48, 128), f32(1056, 128),
            pltpu.SemaphoreType.DMA((7,)),
        ],
        compiler_params=MAIN_PARAMS,
    )(*maps, above, below, cl, cr, c0, c1, block_b2, block_b3, up_w1[0], *ready, *far)
    return (outs[0],) + tuple(o.transpose(2, 0, 1) for o in outs[1:])


def solution(mesh):
    tile = P(None, "ty", "tx")
    return jax.shard_map(
        per_device,
        mesh=mesh,
        in_specs=(tile,) * 4 + (P(),) * 16,
        out_specs=(tile,) * 4,
        check_vma=False,
    )
```

time: 57.1 us -> 47.3 us (0.83)
  Pallas kernels: 34.7 us -> 26.9 us
  waiting for transfers between devices: 7.32 us -> 4.55 us
  local copies, waits for them, and re-layouts: 3.87 us -> 4.58 us
    pallas_call x1, Pallas kernels: 34.1 us -> 24.2 us  [per_device(): pl.pallas_call(main, out_shape=[shape(48, 64, 64), shape(32, 32, 96), sha...]
    ppermute x4, waiting for transfers between devices: 7.32 us -> 4.55 us  [ring(): return lax.ppermute(x, axis, [(i, (i + by) % n) for i in range(n)])]
    pallas_call x0 -> x1, Pallas kernels: none -> 1.53 us  [per_device(): pl.pallas_call(prepare, out_shape=[shape(2, 256, 1536), shape(2, 256, 153...]
    unnamed x20 -> x38, local copies, waits for them, and re-layouts: 3.87 us -> 4.58 us
    pallas_call x1, Pallas kernels: 0.12 us -> 0.78 us  [per_device(): pl.pallas_call(pack_rows, out_shape=[shape(DOWN_ROWS, 128), shape(UP_ROWS...]
  transfers between devices with their start and end apart: 4 -> 4, of which waited for: 4 -> 3; matrix products, arithmetic and copies ran while one was open for 2% -> 3% of each run, Pallas kernels for 0% -> 3%
where the time goes in v2:
time: 47.3 us; the launch traced here: 47.1 us
  Pallas kernels  26.9 us (57%)
  starting transfers between devices  10.2 us (22%)
  local copies, waits for them, and re-layouts  4.58 us (10%)
  waiting for transfers between devices  4.55 us (10%)
  between operations  0.86 us (2%)
    pallas_call x1, Pallas kernels, per_device(): pl.pallas_call(main, out_shape=[shape(48, 64, 64), shape(32, 32, 96), sha...  24.2 us
    ppermute x4, starting transfers between devices, ring(): return lax.ppermute(x, axis, [(i, (i + by) % n) for i in range(n)])  10.2 us
    unnamed x38, local copies, waits for them, and re-layouts  4.58 us
    ppermute x4, waiting for transfers between devices, ring(): return lax.ppermute(x, axis, [(i, (i + by) % n) for i in range(n)])  4.55 us
    pallas_call x1, Pallas kernels, per_device(): pl.pallas_call(prepare, out_shape=[shape(2, 256, 1536), shape(2, 256, 153...  1.53 us
  transfers between devices with their start and end apart: 4, of which 3 were waited for; matrix products, arithmetic and copies ran while one was open for 3% of the time, Pallas kernels for 3%

profile of v2, /device:TPU:4, one launch (start us, length us, event | category | flops | bytes accessed | tf_op | source)
XLA Modules:
  0.0 47.1 jit_solution(11309046644052910353)
XLA Ops:
  0.6 0.0 copy-start.6
  0.6 0.0 copy-start.5
  0.7 0.0 copy-start.1
  0.7 2.0 %copy.24 = bf16[48,64,64]{0,2,1:T(8,128)(2,1)S(1)} copy(bf16[48,64,64]{2,1,0:T(8,128)(2,1)} %param.20) | data formatting | bytes 786432 | tf_op args[0]
  2.7 0.0 copy-done.6
  2.7 0.8 %shard_map.219 = (bf16[592,128]{1,0:T(8,128)(2,1)}, bf16[240,128]{1,0:T(8,128)(2,1)}) custom-call(bf16[64,64,48]{2,1,0:T(8,128)(2,1)S(1)} %bitcast.17, bf16[32,32,96]{2,1,0:T(8,128)(2,1)S(1)} %bitcast.24, bf16[16,16,192]{2,1,0:T(8,128)(2,1)S(1)} %bitcast.28, bf16[8,8,384]{2,1,0:T(8,128)(2,1)S(1)} %bitcast.31), custom_call_target="tpu_custom_call" | custom-call | tf_op jit(solution)/shard_map/pallas_call | solution.py:501
  3.5 1.7 %collective-permute-start = (bf16[592,128]{1,0:T(8,128)(2,1)}, bf16[592,128]{1,0:T(8,128)(2,1)S(1)}, u32[]{:S(2)}, u32[]{:S(2)}) collective-permute-start(bf16[592,128]{1,0:T(8,128)(2,1)} %get-tuple-element.22), channel_id=1, source_target_pairs={{0,8},{8,16},{16,24},{24,32},{32,40},{40,48},{48,56},{56,0},{1,9},... | collective-permute-start | bytes 454664 | tf_op jit(solution)/shard_map/ppermute | solution.py:486
  5.1 2.6 %collective-permute-start.1 = (bf16[240,128]{1,0:T(8,128)(2,1)}, bf16[240,128]{1,0:T(8,128)(2,1)S(1)}, u32[]{:S(2)}, u32[]{:S(2)}) collective-permute-start(bf16[240,128]{1,0:T(8,128)(2,1)} %get-tuple-element.23), channel_id=1, source_target_pairs={{0,56},{8,0},{16,8},{24,16},{32,24},{40,32},{48,40},{56,48},{1,57}... | collective-permute-start | bytes 184328 | tf_op jit(solution)/shard_map/ppermute | solution.py:486
  7.7 1.3 %copy.25 = bf16[1,672,432]{2,1,0:T(8,128)(2,1)S(1)} copy(bf16[1,672,432]{1,2,0:T(8,128)(2,1)} %param.37) | data formatting | bytes 1161216 | tf_op args[17]
  9.0 0.0 copy-start.7
  9.0 0.0 copy-start.9
  9.1 0.0 copy-start.10
  9.1 0.8 %collective-permute-done.1.below = bf16[240,128]{1,0:T(8,128)(2,1)S(1)} collective-permute-done((bf16[240,128]{1,0:T(8,128)(2,1)}, bf16[240,128]{1,0:T(8,128)(2,1)S(1)}, u32[]{:S(2)}, u32[]{:S(2)}) %collective-permute-start.1) | collective-permute-done | bytes 61472 | tf_op jit(solution)/shard_map/ppermute | solution.py:486
  9.9 1.7 %collective-permute-done.above = bf16[592,128]{1,0:T(8,128)(2,1)S(1)} collective-permute-done((bf16[592,128]{1,0:T(8,128)(2,1)}, bf16[592,128]{1,0:T(8,128)(2,1)S(1)}, u32[]{:S(2)}, u32[]{:S(2)}) %collective-permute-start) | collective-permute-done | bytes 151584 | tf_op jit(solution)/shard_map/ppermute | solution.py:486
  11.6 0.4 shard_map.220
  12.0 0.0 copy-start.3
  12.0 0.0 copy-start.8
  12.0 0.0 copy-start.12
  12.0 0.0 copy-start.13
  12.0 0.0 copy-start.14
  12.1 0.0 copy-start.15
  12.1 2.0 %collective-permute-start.2 = (bf16[928,128]{1,0:T(8,128)(2,1)S(1)}, bf16[928,128]{1,0:T(8,128)(2,1)S(1)}, u32[]{:S(2)}, u32[]{:S(2)}) collective-permute-start(bf16[928,128]{1,0:T(8,128)(2,1)S(1)} %get-tuple-element.26), channel_id=1, source_target_pairs={{0,1},{1,2},{2,3},{3,4},{4,5},{5,6},{6,7},{7,0},{8,9},{9,10},{10,1... | collective-permute-start | bytes 712712 | tf_op jit(solution)/shard_map/ppermute | solution.py:486
  14.1 4.0 %collective-permute-start.3 = (bf16[400,128]{1,0:T(8,128)(2,1)S(1)}, bf16[400,128]{1,0:T(8,128)(2,1)S(1)}, u32[]{:S(2)}, u32[]{:S(2)}) collective-permute-start(bf16[400,128]{1,0:T(8,128)(2,1)S(1)} %get-tuple-element.27), channel_id=1, source_target_pairs={{0,7},{1,0},{2,1},{3,2},{4,3},{5,4},{6,5},{7,6},{8,15},{9,8},{10,9... | collective-permute-start | bytes 307208 | tf_op jit(solution)/shard_map/ppermute | solution.py:486
  18.1 0.0 copy-done.11
  18.1 1.5 %shard_map.221 = (bf16[2,256,1536]{2,1,0:T(8,128)(2,1)S(1)}, bf16[2,256,1536]{2,1,0:T(8,128)(2,1)S(1)}, f32[2,256]{1,0:T(2,128)S(1)}, f32[2,256]{1,0:T(2,128)S(1...) custom-call(bf16[2,48,432]{2,1,0:T(8,128)(2,1)S(1)} %copy-done.11, ...), custom_call_target="tpu_custom_call" | custom-call | tf_op jit(solution)/shard_map/pallas_call | solution.py:517
  19.7 0.0 copy-start.2
  19.7 1.2 %copy-done.2 = bf16[2,256,1536]{2,1,0:T(8,128)(2,1)} copy-done((bf16[2,256,1536]{2,1,0:T(8,128)(2,1)}, bf16[2,256,1536]{2,1,0:T(8,128)(2,1)S(1)}, u32[]{:S(2)}) %copy-start.2) | copy-done | bytes 1572888
  20.8 0.0 collective-permute-done.3.cr
  20.8 2.1 %collective-permute-done.2.cl = bf16[928,128]{1,0:T(8,128)(2,1)S(1)} collective-permute-done((bf16[928,128]{1,0:T(8,128)(2,1)S(1)}, bf16[928,128]{1,0:T(8,128)(2,1)S(1)}, u32[]{:S(2)}, u32[]{:S(2)}) %collective-permute-start.2) | collective-permute-done | bytes 237600 | tf_op jit(solution)/shard_map/ppermute | solution.py:486
  22.9 0.0 copy-done.4
  22.9 0.0 copy-done.8
  23.0 24.2 %shard_map.222 = (bf16[48,64,64]{2,1,0:T(8,128)(2,1)}, bf16[32,32,96]{2,1,0:T(8,128)(2,1)}, bf16[16,16,192]{2,1,0:T(8,128)(2,1)}, bf16[8,8,384]{2,1,0:T(8,128)(2,1)}) custom-call(bf16[64,64,48]{2,1,0:T(8,128)(2,1)S(1)} %bitcast.19, bf16[32,32,96]{2,1,0:T(8,128)(2,1)S(1)} %bitcast.26, bf16[16,16,192]{2,1,0:T(8,128)(2,1)S(1)} %bitcast.30, ...), custom_call_target="tpu_custom_call" | custom-call | tf_op jit(solution)/shard_map/pallas_call | solution.py:531
  (18 shorter events, 0.0 us)
Async XLA Ops:
  0.6 2.0 %copy-start.6 = (bf16[384,8,8]{0,2,1:T(8,128)(2,1)S(1)}, bf16[384,8,8]{0,2,1:T(8,128)(2,1)}, u32[]{:S(2)}) copy-start(bf16[384,8,8]{0,2,1:T(8,128)(2,1)} %param.23) | copy-start | bytes 147460
  0.6 2.0 %copy-start.5 = (bf16[192,16,16]{0,2,1:T(8,128)(2,1)S(1)}, bf16[192,16,16]{0,2,1:T(8,128)(2,1)}, u32[]{:S(2)}) copy-start(bf16[192,16,16]{0,2,1:T(8,128)(2,1)} %param.22) | copy-start | bytes 294916
  0.7 2.0 %copy-start.1 = (bf16[96,32,32]{0,2,1:T(8,128)(2,1)S(1)}, bf16[96,32,32]{0,2,1:T(8,128)(2,1)}, u32[]{:S(2)}) copy-start(bf16[96,32,32]{0,2,1:T(8,128)(2,1)} %param.21) | copy-start | bytes 589828
  3.5 14.6 %copy-start = (bf16[1,576,864]{2,1,0:T(8,128)(2,1)S(1)}, bf16[1,576,864]{2,1,0:T(8,128)(2,1)}, u32[]{:S(2)}) copy-start(bf16[1,576,864]{2,1,0:T(8,128)(2,1)} %param.38) | copy-start | bytes 2985988
  3.5 14.6 %copy-start.11 = (bf16[2,48,432]{2,1,0:T(8,128)(2,1)S(1)}, bf16[2,48,432]{2,1,0:T(8,128)(2,1)}, u32[]{:S(2)}) copy-start(bf16[2,48,432]{2,1,0:T(8,128)(2,1)} %w0.1) | copy-start | bytes 248836
  3.5 14.6 %copy-start.16 = (f32[2,48]{1,0:T(2,128)S(1)}, f32[2,48]{1,0:T(2,128)}, u32[]{:S(2)}) copy-start(f32[2,48]{1,0:T(2,128)} %b0.1) | copy-start | bytes 1156
  3.5 14.6 %copy-start.17 = (f32[2,96]{1,0:T(2,128)S(1)}, f32[2,96]{1,0:T(2,128)}, u32[]{:S(2)}) copy-start(f32[2,96]{1,0:T(2,128)} %b1.1) | copy-start | bytes 2308
  3.5 8.1 %collective-permute-start = (bf16[592,128]{1,0:T(8,128)(2,1)}, bf16[592,128]{1,0:T(8,128)(2,1)S(1)}, u32[]{:S(2)}, u32[]{:S(2)}) collective-permute-start(bf16[592,128]{1,0:T(8,128)(2,1)} %get-tuple-element.22), channel_id=1, source_target_pairs={{0,8},{8,16},{16,24},{24,32},{32,40},{40,48},{48,56},{56,0},{1,9},... | collective-permute-start | bytes 454664 | tf_op jit(solution)/shard_map/ppermute | solution.py:486
  5.1 4.7 %collective-permute-start.1 = (bf16[240,128]{1,0:T(8,128)(2,1)}, bf16[240,128]{1,0:T(8,128)(2,1)S(1)}, u32[]{:S(2)}, u32[]{:S(2)}) collective-permute-start(bf16[240,128]{1,0:T(8,128)(2,1)} %get-tuple-element.23), channel_id=1, source_target_pairs={{0,56},{8,0},{16,8},{24,16},{32,24},{40,32},{48,40},{56,48},{1,57}... | collective-permute-start | bytes 184328 | tf_op jit(solution)/shard_map/ppermute | solution.py:486
  9.0 9.1 %copy-start.7 = (bf16[2,96,864]{2,1,0:T(8,128)(2,1)S(1)}, bf16[2,96,864]{2,1,0:T(8,128)(2,1)}, u32[]{:S(2)}) copy-start(bf16[2,96,864]{2,1,0:T(8,128)(2,1)} %w1.1) | copy-start | bytes 995332
  9.0 9.1 %copy-start.9 = (bf16[1,1,96,864]{3,2,1,0:T(8,128)(2,1)S(1)}, bf16[1,1,96,864]{3,2,1,0:T(8,128)(2,1)}, u32[]{:S(2)}) copy-start(bf16[1,1,96,864]{3,2,1,0:T(8,128)(2,1)} %param.36) | copy-start | bytes 497668
  9.1 9.1 %copy-start.10 = (bf16[1,3,48,432]{3,2,1,0:T(8,128)(2,1)S(1)}, bf16[1,3,48,432]{3,2,1,0:T(8,128)(2,1)}, u32[]{:S(2)}) copy-start(bf16[1,3,48,432]{3,2,1,0:T(8,128)(2,1)} %param.35) | copy-start | bytes 373252
  11.6 11.4 %copy-start.4 = (bf16[1,384,1728]{1,2,0:T(8,128)(2,1)S(1)}, bf16[1,384,1728]{1,2,0:T(8,128)(2,1)}, u32[]{:S(2)}) copy-start(bf16[1,384,1728]{1,2,0:T(8,128)(2,1)} %param.39) | copy-start | bytes 3981316
  12.0 10.9 %copy-start.3 = (bf16[2,192,1728]{2,1,0:T(8,128)(2,1)S(1)}, bf16[2,192,1728]{2,1,0:T(8,128)(2,1)}, u32[]{:S(2)}) copy-start(bf16[2,192,1728]{2,1,0:T(8,128)(2,1)} %rest_5_.1) | copy-start | bytes 3981316
  12.0 10.9 %copy-start.8 = (bf16[1,336,384]{2,1,0:T(8,128)(2,1)S(1)}, bf16[1,336,384]{2,1,0:T(8,128)(2,1)}, u32[]{:S(2)}) copy-start(bf16[1,336,384]{2,1,0:T(8,128)(2,1)} %param.34) | copy-start | bytes 774148
  12.0 10.9 %copy-start.12 = (bf16[1,144,192]{2,1,0:T(8,128)(2,1)S(1)}, bf16[1,144,192]{2,1,0:T(8,128)(2,1)}, u32[]{:S(2)}) copy-start(bf16[1,144,192]{2,1,0:T(8,128)(2,1)} %param.33) | copy-start | bytes 165892
  12.0 10.9 %copy-start.13 = (bf16[1,48,96]{2,1,0:T(8,128)(2,1)S(1)}, bf16[1,48,96]{2,1,0:T(8,128)(2,1)}, u32[]{:S(2)}) copy-start(bf16[1,48,96]{2,1,0:T(8,128)(2,1)} %param.32) | copy-start | bytes 27652
  12.0 10.9 %copy-start.14 = (f32[2,384]{1,0:T(2,128)S(1)}, f32[2,384]{1,0:T(2,128)}, u32[]{:S(2)}) copy-start(f32[2,384]{1,0:T(2,128)} %b3.1) | copy-start | bytes 9220
  12.1 10.9 %copy-start.15 = (f32[2,192]{1,0:T(2,128)S(1)}, f32[2,192]{1,0:T(2,128)}, u32[]{:S(2)}) copy-start(f32[2,192]{1,0:T(2,128)} %b2.1) | copy-start | bytes 4612
  12.1 10.8 %collective-permute-start.2 = (bf16[928,128]{1,0:T(8,128)(2,1)S(1)}, bf16[928,128]{1,0:T(8,128)(2,1)S(1)}, u32[]{:S(2)}, u32[]{:S(2)}) collective-permute-start(bf16[928,128]{1,0:T(8,128)(2,1)S(1)} %get-tuple-element.26), channel_id=1, source_target_pairs={{0,1},{1,2},{2,3},{3,4},{4,5},{5,6},{6,7},{7,0},{8,9},{9,10},{10,1... | collective-permute-start | bytes 712712 | tf_op jit(solution)/shard_map/ppermute | solution.py:486
  14.1 6.8 %collective-permute-start.3 = (bf16[400,128]{1,0:T(8,128)(2,1)S(1)}, bf16[400,128]{1,0:T(8,128)(2,1)S(1)}, u32[]{:S(2)}, u32[]{:S(2)}) collective-permute-start(bf16[400,128]{1,0:T(8,128)(2,1)S(1)} %get-tuple-element.27), channel_id=1, source_target_pairs={{0,7},{1,0},{2,1},{3,2},{4,3},{5,4},{6,5},{7,6},{8,15},{9,8},{10,9... | collective-permute-start | bytes 307208 | tf_op jit(solution)/shard_map/ppermute | solution.py:486
  19.7 1.2 %copy-start.2 = (bf16[2,256,1536]{2,1,0:T(8,128)(2,1)}, bf16[2,256,1536]{2,1,0:T(8,128)(2,1)S(1)}, u32[]{:S(2)}) copy-start(bf16[2,256,1536]{2,1,0:T(8,128)(2,1)S(1)} %get-tuple-element.32.rest_1_) | copy-start | bytes 4718596

commit v3 on v2

--- a/solution.py
+++ b/solution.py
@@ -19,7 +19,7 @@
 DOWN_ROWS, UP_ROWS = 592, 240
 RIGHT_ROWS, LEFT_ROWS = 928, 400
 PARAMS = pltpu.CompilerParams(vmem_limit_bytes=16 * 2**20)
-MAIN_PARAMS = pltpu.CompilerParams(vmem_limit_bytes=44 * 2**20)
+MAIN_PARAMS = pltpu.CompilerParams(vmem_limit_bytes=39 * 2**20)
 
 
 def spans(chan):
@@ -178,8 +178,8 @@
 
 
 def main(f0, f1, f2, f3, above, below, cl, cr, b0, b1, b2, b3, u1, *rest):
-    ready, far, rest = rest[:5], rest[5:12], rest[12:]
-    outs, near, scratch = rest[:4], rest[4:11], rest[11:-1]
+    ready, far, rest = rest[:11], rest[11:12], rest[12:]
+    outs, near, scratch = rest[:4], rest[4:5], rest[5:-1]
     main_body(
         f0, f1, f2, f3, above, below, cl, cr, b0, b1, b2, b3, u1, ready, far, near, rest[-1], *outs, *scratch
     )
@@ -197,8 +197,8 @@
     copies = [pltpu.make_async_copy(a, b, sems.at[i]) for i, (a, b) in enumerate(zip(far, near))]
     for copy in copies:
         copy.start()
-    q0, q1, d01, d02, d12 = ready
-    w2, w3, fin0, fin1, fin2, u3, u2 = near
+    q0, q1, d01, d02, d12, fin0, fin1, fin2, u3, u2, w2 = ready
+    w3 = near[0]
     place = (lax.axis_index("ty"), lax.axis_index("tx"))
     feats = (f0, f1, f2, f3)
     two = lambda ref: [ref.at[0], ref.at[1]]
@@ -340,14 +340,11 @@
         steps(outer_rows, counts[3], outer)
         clear_edges(place, as_[b], per, pitch, EXT[b] - 4, EXT[b] - 4, lead - 2, 0)
 
-    block(0, q0, b0, s0, (5, 5, 5, 5))
-    block(1, q1, b1, s1, (3, 3, 3, 3))
+    block(0, q0, b0, s0, (1, 1, 1, 1))
+    block(1, q1, b1, s1, (1, 1, 1, 1))
+    block(2, w2, b2, s2, (1, 1, 1, 1))
     copies[0].wait()
-    block(2, w2, b2, s2, (1, 2, 1, 2))
-    copies[1].wait()
     block(3, w3, b3, s3, (1, 1, 1, 1))
-    for copy in copies[2:]:
-        copy.wait()
 
     for pair in range(36):
         for dx in range(3):
@@ -526,12 +523,12 @@
     vmem = pl.BlockSpec(memory_space=pltpu.VMEM)
     f32 = lambda *dims: pltpu.VMEM(dims, F32)
     bf = lambda *dims: pltpu.VMEM(dims, BF)
-    ready = (q0, q1, d01, d02, d12)
-    far = (block_w2, block_w3, fin0, fin1, down_fin2[0].T, up_w3[0], up_w2[0])
+    ready = (q0, q1, d01, d02, d12, fin0, fin1, down_fin2[0].T, up_w3[0], up_w2[0], block_w2)
+    far = (block_w3,)
     outs = pl.pallas_call(
         main,
         out_shape=[shape(48, 64, 64), shape(32, 32, 96), shape(16, 16, 192), shape(8, 8, 384)],
-        in_specs=[vmem] * 18 + [pl.BlockSpec(memory_space=pltpu.HBM)] * 7,
+        in_specs=[vmem] * 24 + [pl.BlockSpec(memory_space=pltpu.HBM)],
         scratch_shapes=[bf(*w.shape) for w in far]
         + [
             f32(2, 1616, 128), f32(2, 1536, 128), f32(2, 1536, 128), bf(1600, 768), bf(1728, 384),
@@ -542,7 +539,7 @@
             f32(3, 208, 128), f32(3, 176, 128), f32(3, 128, 128), bf(192, 1152),
             f32(1024, 48), f32(256, 48), f32(256, 96), f32(1024, 96), f32(256, 128),
             bf(1024, 96), f32(4, 64, 128), f32(3840, 64), f32(80, 48), f32(2, 2, 48, 128), f32(1056, 128),
-            pltpu.SemaphoreType.DMA((7,)),
+            pltpu.SemaphoreType.DMA((1,)),
         ],
         compiler_params=MAIN_PARAMS,
     )(*maps, above, below, cl, cr, c0, c1, block_b2, block_b3, up_w1[0], *ready, *far)

time: 47.3 us -> 44.9 us (0.949)
  Pallas kernels: 26.9 us -> 24.4 us
  local copies, waits for them, and re-layouts: 4.58 us -> 3.41 us
  waiting for transfers between devices: 4.55 us -> 5.72 us
    pallas_call x1, Pallas kernels: 24.2 us -> 21.6 us  [per_device(): pl.pallas_call(main, out_shape=[shape(48, 64, 64), shape(32, 32, 96), sha...]
    ppermute x4, waiting for transfers between devices: 4.55 us -> 5.72 us  [ring(): return lax.ppermute(x, axis, [(i, (i + by) % n) for i in range(n)])]
    unnamed x38 -> x36, local copies, waits for them, and re-layouts: 4.58 us -> 3.41 us
  transfers between devices with their start and end apart: 4 -> 4, of which waited for: 3 -> 4; matrix products, arithmetic and copies ran while one was open for 3% -> 3% of each run, Pallas kernels for 3% -> 3%
where the time goes in v3:
time: 44.9 us; the launch traced here: 44.7 us
  Pallas kernels  24.4 us (54%)
  starting transfers between devices  10.2 us (23%)
  waiting for transfers between devices  5.72 us (13%)
  local copies, waits for them, and re-layouts  3.41 us (8%)
  between operations  1.01 us (2%)
    pallas_call x1, Pallas kernels, per_device(): pl.pallas_call(main, out_shape=[shape(48, 64, 64), shape(32, 32, 96), sha...  21.6 us
    ppermute x4, starting transfers between devices, ring(): return lax.ppermute(x, axis, [(i, (i + by) % n) for i in range(n)])  10.2 us
    ppermute x4, waiting for transfers between devices, ring(): return lax.ppermute(x, axis, [(i, (i + by) % n) for i in range(n)])  5.72 us
    unnamed x36, local copies, waits for them, and re-layouts  3.41 us
    pallas_call x1, Pallas kernels, per_device(): pl.pallas_call(prepare, out_shape=[shape(2, 256, 1536), shape(2, 256, 153...  1.53 us
  transfers between devices with their start and end apart: 4, of which 4 were waited for; matrix products, arithmetic and copies ran while one was open for 3% of the time, Pallas kernels for 3%

profile of v3, /device:TPU:4, one launch (start us, length us, event | category | flops | bytes accessed | tf_op | source)
XLA Modules:
  0.0 44.7 jit_solution(8101892580519175019)
XLA Ops:
  0.6 0.0 copy-start.5
  0.6 0.0 copy-start.4
  0.7 0.0 copy-start.1
  0.7 2.0 %copy.24 = bf16[48,64,64]{0,2,1:T(8,128)(2,1)S(1)} copy(bf16[48,64,64]{2,1,0:T(8,128)(2,1)} %param.20) | data formatting | bytes 786432 | tf_op args[0]
  2.7 0.0 copy-done.5
  2.7 0.0 copy-done.4
  2.7 0.0 copy-done.1
  2.7 0.8 %shard_map.219 = (bf16[592,128]{1,0:T(8,128)(2,1)}, bf16[240,128]{1,0:T(8,128)(2,1)}) custom-call(bf16[64,64,48]{2,1,0:T(8,128)(2,1)S(1)} %bitcast.17, bf16[32,32,96]{2,1,0:T(8,128)(2,1)S(1)} %bitcast.24, bf16[16,16,192]{2,1,0:T(8,128)(2,1)S(1)} %bitcast.28, bf16[8,8,384]{2,1,0:T(8,128)(2,1)S(1)} %bitcast.31), custom_call_target="tpu_custom_call" | custom-call | tf_op jit(solution)/shard_map/pallas_call | solution.py:498
  3.5 1.7 %collective-permute-start = (bf16[592,128]{1,0:T(8,128)(2,1)}, bf16[592,128]{1,0:T(8,128)(2,1)S(1)}, u32[]{:S(2)}, u32[]{:S(2)}) collective-permute-start(bf16[592,128]{1,0:T(8,128)(2,1)} %get-tuple-element.22), channel_id=1, source_target_pairs={{0,8},{8,16},{16,24},{24,32},{32,40},{40,48},{48,56},{56,0},{1,9},... | collective-permute-start | bytes 454664 | tf_op jit(solution)/shard_map/ppermute | solution.py:483
  5.1 2.6 %collective-permute-start.1 = (bf16[240,128]{1,0:T(8,128)(2,1)}, bf16[240,128]{1,0:T(8,128)(2,1)S(1)}, u32[]{:S(2)}, u32[]{:S(2)}) collective-permute-start(bf16[240,128]{1,0:T(8,128)(2,1)} %get-tuple-element.23), channel_id=1, source_target_pairs={{0,56},{8,0},{16,8},{24,16},{32,24},{40,32},{48,40},{56,48},{1,57}... | collective-permute-start | bytes 184328 | tf_op jit(solution)/shard_map/ppermute | solution.py:483
  7.7 1.3 %copy.25 = bf16[1,672,432]{2,1,0:T(8,128)(2,1)S(1)} copy(bf16[1,672,432]{1,2,0:T(8,128)(2,1)} %param.37) | data formatting | bytes 1161216 | tf_op args[17]
  9.0 0.0 copy-start.6
  9.0 0.0 copy-start.8
  9.1 0.0 copy-start.9
  9.1 0.8 %collective-permute-done.1.below = bf16[240,128]{1,0:T(8,128)(2,1)S(1)} collective-permute-done((bf16[240,128]{1,0:T(8,128)(2,1)}, bf16[240,128]{1,0:T(8,128)(2,1)S(1)}, u32[]{:S(2)}, u32[]{:S(2)}) %collective-permute-start.1) | collective-permute-done | bytes 61472 | tf_op jit(solution)/shard_map/ppermute | solution.py:483
  9.9 1.7 %collective-permute-done.above = bf16[592,128]{1,0:T(8,128)(2,1)S(1)} collective-permute-done((bf16[592,128]{1,0:T(8,128)(2,1)}, bf16[592,128]{1,0:T(8,128)(2,1)S(1)}, u32[]{:S(2)}, u32[]{:S(2)}) %collective-permute-start) | collective-permute-done | bytes 151584 | tf_op jit(solution)/shard_map/ppermute | solution.py:483
  11.6 0.4 shard_map.220
  12.0 0.0 copy-start.2
  12.0 0.0 copy-start.7
  12.0 0.0 copy-start.11
  12.0 0.0 copy-start.12
  12.0 0.0 copy-start.13
  12.1 0.0 copy-start.14
  12.1 2.0 %collective-permute-start.2 = (bf16[928,128]{1,0:T(8,128)(2,1)S(1)}, bf16[928,128]{1,0:T(8,128)(2,1)S(1)}, u32[]{:S(2)}, u32[]{:S(2)}) collective-permute-start(bf16[928,128]{1,0:T(8,128)(2,1)S(1)} %get-tuple-element.26), channel_id=1, source_target_pairs={{0,1},{1,2},{2,3},{3,4},{4,5},{5,6},{6,7},{7,0},{8,9},{9,10},{10,1... | collective-permute-start | bytes 712712 | tf_op jit(solution)/shard_map/ppermute | solution.py:483
  14.1 4.0 %collective-permute-start.3 = (bf16[400,128]{1,0:T(8,128)(2,1)S(1)}, bf16[400,128]{1,0:T(8,128)(2,1)S(1)}, u32[]{:S(2)}, u32[]{:S(2)}) collective-permute-start(bf16[400,128]{1,0:T(8,128)(2,1)S(1)} %get-tuple-element.27), channel_id=1, source_target_pairs={{0,7},{1,0},{2,1},{3,2},{4,3},{5,4},{6,5},{7,6},{8,15},{9,8},{10,9... | collective-permute-start | bytes 307208 | tf_op jit(solution)/shard_map/ppermute | solution.py:483
  18.1 0.0 copy-done
  18.1 0.0 copy-done.6
  18.1 0.0 copy-done.8
  18.1 1.5 %shard_map.221 = (bf16[2,256,1536]{2,1,0:T(8,128)(2,1)S(1)}, bf16[2,256,1536]{2,1,0:T(8,128)(2,1)S(1)}, f32[2,256]{1,0:T(2,128)S(1)}, f32[2,256]{1,0:T(2,128)S(1...) custom-call(bf16[2,48,432]{2,1,0:T(8,128)(2,1)S(1)} %copy-done.10, ...), custom_call_target="tpu_custom_call" | custom-call | tf_op jit(solution)/shard_map/pallas_call | solution.py:514
  19.7 0.7 %collective-permute-done.3.cr = bf16[400,128]{1,0:T(8,128)(2,1)S(1)} collective-permute-done((bf16[400,128]{1,0:T(8,128)(2,1)S(1)}, bf16[400,128]{1,0:T(8,128)(2,1)S(1)}, u32[]{:S(2)}, u32[]{:S(2)}) %collective-permute-start.3) | collective-permute-done | bytes 102432 | tf_op jit(solution)/shard_map/ppermute | solution.py:483
  20.3 2.6 %collective-permute-done.2.cl = bf16[928,128]{1,0:T(8,128)(2,1)S(1)} collective-permute-done((bf16[928,128]{1,0:T(8,128)(2,1)S(1)}, bf16[928,128]{1,0:T(8,128)(2,1)S(1)}, u32[]{:S(2)}, u32[]{:S(2)}) %collective-permute-start.2) | collective-permute-done | bytes 237600 | tf_op jit(solution)/shard_map/ppermute | solution.py:483
  23.0 21.6 %shard_map.222 = (bf16[48,64,64]{2,1,0:T(8,128)(2,1)}, bf16[32,32,96]{2,1,0:T(8,128)(2,1)}, bf16[16,16,192]{2,1,0:T(8,128)(2,1)}, bf16[8,8,384]{2,1,0:T(8,128)(2,1)}) custom-call(bf16[64,64,48]{2,1,0:T(8,128)(2,1)S(1)} %bitcast.19, bf16[32,32,96]{2,1,0:T(8,128)(2,1)S(1)} %bitcast.26, bf16[16,16,192]{2,1,0:T(8,128)(2,1)S(1)} %bitcast.30, ...), custom_call_target="tpu_custom_call" | custom-call | tf_op jit(solution)/shard_map/pallas_call | solution.py:528
  (16 shorter events, 0.0 us)
Async XLA Ops:
  0.6 2.0 %copy-start.5 = (bf16[384,8,8]{0,2,1:T(8,128)(2,1)S(1)}, bf16[384,8,8]{0,2,1:T(8,128)(2,1)}, u32[]{:S(2)}) copy-start(bf16[384,8,8]{0,2,1:T(8,128)(2,1)} %param.23) | copy-start | bytes 147460
  0.6 2.0 %copy-start.4 = (bf16[192,16,16]{0,2,1:T(8,128)(2,1)S(1)}, bf16[192,16,16]{0,2,1:T(8,128)(2,1)}, u32[]{:S(2)}) copy-start(bf16[192,16,16]{0,2,1:T(8,128)(2,1)} %param.22) | copy-start | bytes 294916
  0.7 2.0 %copy-start.1 = (bf16[96,32,32]{0,2,1:T(8,128)(2,1)S(1)}, bf16[96,32,32]{0,2,1:T(8,128)(2,1)}, u32[]{:S(2)}) copy-start(bf16[96,32,32]{0,2,1:T(8,128)(2,1)} %param.21) | copy-start | bytes 589828
  3.5 14.6 %copy-start = (bf16[1,576,864]{2,1,0:T(8,128)(2,1)S(1)}, bf16[1,576,864]{2,1,0:T(8,128)(2,1)}, u32[]{:S(2)}) copy-start(bf16[1,576,864]{2,1,0:T(8,128)(2,1)} %param.38) | copy-start | bytes 2985988
  3.5 14.6 %copy-start.10 = (bf16[2,48,432]{2,1,0:T(8,128)(2,1)S(1)}, bf16[2,48,432]{2,1,0:T(8,128)(2,1)}, u32[]{:S(2)}) copy-start(bf16[2,48,432]{2,1,0:T(8,128)(2,1)} %w0.1) | copy-start | bytes 248836
  3.5 14.6 %copy-start.15 = (f32[2,48]{1,0:T(2,128)S(1)}, f32[2,48]{1,0:T(2,128)}, u32[]{:S(2)}) copy-start(f32[2,48]{1,0:T(2,128)} %b0.1) | copy-start | bytes 1156
  3.5 14.6 %copy-start.16 = (f32[2,96]{1,0:T(2,128)S(1)}, f32[2,96]{1,0:T(2,128)}, u32[]{:S(2)}) copy-start(f32[2,96]{1,0:T(2,128)} %b1.1) | copy-start | bytes 2308
  3.5 8.1 %collective-permute-start = (bf16[592,128]{1,0:T(8,128)(2,1)}, bf16[592,128]{1,0:T(8,128)(2,1)S(1)}, u32[]{:S(2)}, u32[]{:S(2)}) collective-permute-start(bf16[592,128]{1,0:T(8,128)(2,1)} %get-tuple-element.22), channel_id=1, source_target_pairs={{0,8},{8,16},{16,24},{24,32},{32,40},{40,48},{48,56},{56,0},{1,9},... | collective-permute-start | bytes 454664 | tf_op jit(solution)/shard_map/ppermute | solution.py:483
  5.1 4.7 %collective-permute-start.1 = (bf16[240,128]{1,0:T(8,128)(2,1)}, bf16[240,128]{1,0:T(8,128)(2,1)S(1)}, u32[]{:S(2)}, u32[]{:S(2)}) collective-permute-start(bf16[240,128]{1,0:T(8,128)(2,1)} %get-tuple-element.23), channel_id=1, source_target_pairs={{0,56},{8,0},{16,8},{24,16},{32,24},{40,32},{48,40},{56,48},{1,57}... | collective-permute-start | bytes 184328 | tf_op jit(solution)/shard_map/ppermute | solution.py:483
  9.0 9.1 %copy-start.6 = (bf16[2,96,864]{2,1,0:T(8,128)(2,1)S(1)}, bf16[2,96,864]{2,1,0:T(8,128)(2,1)}, u32[]{:S(2)}) copy-start(bf16[2,96,864]{2,1,0:T(8,128)(2,1)} %w1.1) | copy-start | bytes 995332
  9.0 9.1 %copy-start.8 = (bf16[1,1,96,864]{3,2,1,0:T(8,128)(2,1)S(1)}, bf16[1,1,96,864]{3,2,1,0:T(8,128)(2,1)}, u32[]{:S(2)}) copy-start(bf16[1,1,96,864]{3,2,1,0:T(8,128)(2,1)} %param.36) | copy-start | bytes 497668
  9.1 9.1 %copy-start.9 = (bf16[1,3,48,432]{3,2,1,0:T(8,128)(2,1)S(1)}, bf16[1,3,48,432]{3,2,1,0:T(8,128)(2,1)}, u32[]{:S(2)}) copy-start(bf16[1,3,48,432]{3,2,1,0:T(8,128)(2,1)} %param.35) | copy-start | bytes 373252
  11.6 11.4 %copy-start.3 = (bf16[1,384,1728]{1,2,0:T(8,128)(2,1)S(1)}, bf16[1,384,1728]{1,2,0:T(8,128)(2,1)}, u32[]{:S(2)}) copy-start(bf16[1,384,1728]{1,2,0:T(8,128)(2,1)} %param.39) | copy-start | bytes 3981316
  12.0 10.9 %copy-start.2 = (bf16[2,192,1728]{2,1,0:T(8,128)(2,1)S(1)}, bf16[2,192,1728]{2,1,0:T(8,128)(2,1)}, u32[]{:S(2)}) copy-start(bf16[2,192,1728]{2,1,0:T(8,128)(2,1)} %rest_10_.1) | copy-start | bytes 3981316
  12.0 10.9 %copy-start.7 = (bf16[1,336,384]{2,1,0:T(8,128)(2,1)S(1)}, bf16[1,336,384]{2,1,0:T(8,128)(2,1)}, u32[]{:S(2)}) copy-start(bf16[1,336,384]{2,1,0:T(8,128)(2,1)} %param.34) | copy-start | bytes 774148
  12.0 10.9 %copy-start.11 = (bf16[1,144,192]{2,1,0:T(8,128)(2,1)S(1)}, bf16[1,144,192]{2,1,0:T(8,128)(2,1)}, u32[]{:S(2)}) copy-start(bf16[1,144,192]{2,1,0:T(8,128)(2,1)} %param.33) | copy-start | bytes 165892
  12.0 10.9 %copy-start.12 = (bf16[1,48,96]{2,1,0:T(8,128)(2,1)S(1)}, bf16[1,48,96]{2,1,0:T(8,128)(2,1)}, u32[]{:S(2)}) copy-start(bf16[1,48,96]{2,1,0:T(8,128)(2,1)} %param.32) | copy-start | bytes 27652
  12.0 10.9 %copy-start.13 = (f32[2,384]{1,0:T(2,128)S(1)}, f32[2,384]{1,0:T(2,128)}, u32[]{:S(2)}) copy-start(f32[2,384]{1,0:T(2,128)} %b3.1) | copy-start | bytes 9220
  12.1 10.9 %copy-start.14 = (f32[2,192]{1,0:T(2,128)S(1)}, f32[2,192]{1,0:T(2,128)}, u32[]{:S(2)}) copy-start(f32[2,192]{1,0:T(2,128)} %b2.1) | copy-start | bytes 4612
  12.1 10.8 %collective-permute-start.2 = (bf16[928,128]{1,0:T(8,128)(2,1)S(1)}, bf16[928,128]{1,0:T(8,128)(2,1)S(1)}, u32[]{:S(2)}, u32[]{:S(2)}) collective-permute-start(bf16[928,128]{1,0:T(8,128)(2,1)S(1)} %get-tuple-element.26), channel_id=1, source_target_pairs={{0,1},{1,2},{2,3},{3,4},{4,5},{5,6},{6,7},{7,0},{8,9},{9,10},{10,1... | collective-permute-start | bytes 712712 | tf_op jit(solution)/shard_map/ppermute | solution.py:483
  14.1 6.3 %collective-permute-start.3 = (bf16[400,128]{1,0:T(8,128)(2,1)S(1)}, bf16[400,128]{1,0:T(8,128)(2,1)S(1)}, u32[]{:S(2)}, u32[]{:S(2)}) collective-permute-start(bf16[400,128]{1,0:T(8,128)(2,1)S(1)} %get-tuple-element.27), channel_id=1, source_target_pairs={{0,7},{1,0},{2,1},{3,2},{4,3},{5,4},{6,5},{7,6},{8,15},{9,8},{10,9... | collective-permute-start | bytes 307208 | tf_op jit(solution)/shard_map/ppermute | solution.py:483

commit v4 on v3

--- a/solution.py
+++ b/solution.py
@@ -357,7 +357,7 @@
         v01[pl.ds(p, step), :] = rounded(total[:, :128])
         v0[pl.ds(p, step), :] = rounded(jnp.maximum(total[:, 128:], 0.0))
 
-    steps(35 * 48, 5, first)
+    steps(35 * 48, 1, first)
     clear_edges(place, [v0], 1, 48, 35, 35, 3, 0)
 
     for row in range(35):
@@ -459,7 +459,7 @@
         jt[pl.ds(2 * m + 7, 48, stride=80), :] = turned[0:48]
         jt[pl.ds(2 * m + 8, 48, stride=80), :] = turned[64:112]
 
-    @pl.loop(0, 8)
+    @pl.loop(0, 8, unroll=8)
     def _(i):
         for k in range(4):
             y = 4 * i + k
@@ -471,7 +471,7 @@
 
     last_rows(32, 1, 17, 0)
 
-    @pl.loop(0, 6)
+    @pl.loop(0, 6, unroll=6)
     def _(i):
         for c in range(8):
             c = 8 * i + c

time: 44.9 us -> 44.3 us (0.987)
  Pallas kernels: 24.4 us -> 23.8 us
    pallas_call x1, Pallas kernels: 21.6 us -> 21 us  [per_device(): pl.pallas_call(main, out_shape=[shape(48, 64, 64), shape(32, 32, 96), sha...]
where the time goes in v4:
time: 44.3 us; the launch traced here: 44.1 us
  Pallas kernels  23.8 us (54%)
  starting transfers between devices  10.2 us (23%)
  waiting for transfers between devices  5.72 us (13%)
  local copies, waits for them, and re-layouts  3.41 us (8%)
  between operations  1.01 us (2%)
    pallas_call x1, Pallas kernels, per_device(): pl.pallas_call(main, out_shape=[shape(48, 64, 64), shape(32, 32, 96), sha...  21 us
    ppermute x4, starting transfers between devices, ring(): return lax.ppermute(x, axis, [(i, (i + by) % n) for i in range(n)])  10.2 us
    ppermute x4, waiting for transfers between devices, ring(): return lax.ppermute(x, axis, [(i, (i + by) % n) for i in range(n)])  5.72 us
    unnamed x36, local copies, waits for them, and re-layouts  3.41 us
    pallas_call x1, Pallas kernels, per_device(): pl.pallas_call(prepare, out_shape=[shape(2, 256, 1536), shape(2, 256, 153...  1.53 us
  transfers between devices with their start and end apart: 4, of which 4 were waited for; matrix products, arithmetic and copies ran while one was open for 3% of the time, Pallas kernels for 3%

profile of v4, /device:TPU:4, one launch (start us, length us, event | category | flops | bytes accessed | tf_op | source)
XLA Modules:
  0.0 44.1 jit_solution(7070400406000931928)
XLA Ops:
  0.6 0.0 copy-start.5
  0.6 0.0 copy-start.4
  0.7 0.0 copy-start.1
  0.7 2.0 %copy.24 = bf16[48,64,64]{0,2,1:T(8,128)(2,1)S(1)} copy(bf16[48,64,64]{2,1,0:T(8,128)(2,1)} %param.20) | data formatting | bytes 786432 | tf_op args[0]
  2.7 0.0 copy-done.5
  2.7 0.0 copy-done.4
  2.7 0.0 copy-done.1
  2.7 0.8 %shard_map.219 = (bf16[592,128]{1,0:T(8,128)(2,1)}, bf16[240,128]{1,0:T(8,128)(2,1)}) custom-call(bf16[64,64,48]{2,1,0:T(8,128)(2,1)S(1)} %bitcast.17, bf16[32,32,96]{2,1,0:T(8,128)(2,1)S(1)} %bitcast.24, bf16[16,16,192]{2,1,0:T(8,128)(2,1)S(1)} %bitcast.28, bf16[8,8,384]{2,1,0:T(8,128)(2,1)S(1)} %bitcast.31), custom_call_target="tpu_custom_call" | custom-call | tf_op jit(solution)/shard_map/pallas_call | solution.py:498
  3.5 1.7 %collective-permute-start = (bf16[592,128]{1,0:T(8,128)(2,1)}, bf16[592,128]{1,0:T(8,128)(2,1)S(1)}, u32[]{:S(2)}, u32[]{:S(2)}) collective-permute-start(bf16[592,128]{1,0:T(8,128)(2,1)} %get-tuple-element.22), channel_id=1, source_target_pairs={{0,8},{8,16},{16,24},{24,32},{32,40},{40,48},{48,56},{56,0},{1,9},... | collective-permute-start | bytes 454664 | tf_op jit(solution)/shard_map/ppermute | solution.py:483
  5.1 2.6 %collective-permute-start.1 = (bf16[240,128]{1,0:T(8,128)(2,1)}, bf16[240,128]{1,0:T(8,128)(2,1)S(1)}, u32[]{:S(2)}, u32[]{:S(2)}) collective-permute-start(bf16[240,128]{1,0:T(8,128)(2,1)} %get-tuple-element.23), channel_id=1, source_target_pairs={{0,56},{8,0},{16,8},{24,16},{32,24},{40,32},{48,40},{56,48},{1,57}... | collective-permute-start | bytes 184328 | tf_op jit(solution)/shard_map/ppermute | solution.py:483
  7.7 1.3 %copy.25 = bf16[1,672,432]{2,1,0:T(8,128)(2,1)S(1)} copy(bf16[1,672,432]{1,2,0:T(8,128)(2,1)} %param.37) | data formatting | bytes 1161216 | tf_op args[17]
  9.0 0.0 copy-start.6
  9.0 0.0 copy-start.8
  9.1 0.0 copy-start.9
  9.1 0.8 %collective-permute-done.1.below = bf16[240,128]{1,0:T(8,128)(2,1)S(1)} collective-permute-done((bf16[240,128]{1,0:T(8,128)(2,1)}, bf16[240,128]{1,0:T(8,128)(2,1)S(1)}, u32[]{:S(2)}, u32[]{:S(2)}) %collective-permute-start.1) | collective-permute-done | bytes 61472 | tf_op jit(solution)/shard_map/ppermute | solution.py:483
  9.9 1.7 %collective-permute-done.above = bf16[592,128]{1,0:T(8,128)(2,1)S(1)} collective-permute-done((bf16[592,128]{1,0:T(8,128)(2,1)}, bf16[592,128]{1,0:T(8,128)(2,1)S(1)}, u32[]{:S(2)}, u32[]{:S(2)}) %collective-permute-start) | collective-permute-done | bytes 151584 | tf_op jit(solution)/shard_map/ppermute | solution.py:483
  11.6 0.4 shard_map.220
  12.0 0.0 copy-start.2
  12.0 0.0 copy-start.7
  12.0 0.0 copy-start.11
  12.0 0.0 copy-start.12
  12.0 0.0 copy-start.13
  12.1 0.0 copy-start.14
  12.1 2.0 %collective-permute-start.2 = (bf16[928,128]{1,0:T(8,128)(2,1)S(1)}, bf16[928,128]{1,0:T(8,128)(2,1)S(1)}, u32[]{:S(2)}, u32[]{:S(2)}) collective-permute-start(bf16[928,128]{1,0:T(8,128)(2,1)S(1)} %get-tuple-element.26), channel_id=1, source_target_pairs={{0,1},{1,2},{2,3},{3,4},{4,5},{5,6},{6,7},{7,0},{8,9},{9,10},{10,1... | collective-permute-start | bytes 712712 | tf_op jit(solution)/shard_map/ppermute | solution.py:483
  14.1 4.0 %collective-permute-start.3 = (bf16[400,128]{1,0:T(8,128)(2,1)S(1)}, bf16[400,128]{1,0:T(8,128)(2,1)S(1)}, u32[]{:S(2)}, u32[]{:S(2)}) collective-permute-start(bf16[400,128]{1,0:T(8,128)(2,1)S(1)} %get-tuple-element.27), channel_id=1, source_target_pairs={{0,7},{1,0},{2,1},{3,2},{4,3},{5,4},{6,5},{7,6},{8,15},{9,8},{10,9... | collective-permute-start | bytes 307208 | tf_op jit(solution)/shard_map/ppermute | solution.py:483
  18.1 0.0 copy-done
  18.1 0.0 copy-done.6
  18.1 0.0 copy-done.8
  18.1 1.5 %shard_map.221 = (bf16[2,256,1536]{2,1,0:T(8,128)(2,1)S(1)}, bf16[2,256,1536]{2,1,0:T(8,128)(2,1)S(1)}, f32[2,256]{1,0:T(2,128)S(1)}, f32[2,256]{1,0:T(2,128)S(1...) custom-call(bf16[2,48,432]{2,1,0:T(8,128)(2,1)S(1)} %copy-done.10, ...), custom_call_target="tpu_custom_call" | custom-call | tf_op jit(solution)/shard_map/pallas_call | solution.py:514
  19.7 0.7 %collective-permute-done.3.cr = bf16[400,128]{1,0:T(8,128)(2,1)S(1)} collective-permute-done((bf16[400,128]{1,0:T(8,128)(2,1)S(1)}, bf16[400,128]{1,0:T(8,128)(2,1)S(1)}, u32[]{:S(2)}, u32[]{:S(2)}) %collective-permute-start.3) | collective-permute-done | bytes 102432 | tf_op jit(solution)/shard_map/ppermute | solution.py:483
  20.3 2.6 %collective-permute-done.2.cl = bf16[928,128]{1,0:T(8,128)(2,1)S(1)} collective-permute-done((bf16[928,128]{1,0:T(8,128)(2,1)S(1)}, bf16[928,128]{1,0:T(8,128)(2,1)S(1)}, u32[]{:S(2)}, u32[]{:S(2)}) %collective-permute-start.2) | collective-permute-done | bytes 237600 | tf_op jit(solution)/shard_map/ppermute | solution.py:483
  23.0 21.0 %shard_map.222 = (bf16[48,64,64]{2,1,0:T(8,128)(2,1)}, bf16[32,32,96]{2,1,0:T(8,128)(2,1)}, bf16[16,16,192]{2,1,0:T(8,128)(2,1)}, bf16[8,8,384]{2,1,0:T(8,128)(2,1)}) custom-call(bf16[64,64,48]{2,1,0:T(8,128)(2,1)S(1)} %bitcast.19, bf16[32,32,96]{2,1,0:T(8,128)(2,1)S(1)} %bitcast.26, bf16[16,16,192]{2,1,0:T(8,128)(2,1)S(1)} %bitcast.30, ...), custom_call_target="tpu_custom_call" | custom-call | tf_op jit(solution)/shard_map/pallas_call | solution.py:528
  (16 shorter events, 0.0 us)
Async XLA Ops:
  0.6 2.0 %copy-start.5 = (bf16[384,8,8]{0,2,1:T(8,128)(2,1)S(1)}, bf16[384,8,8]{0,2,1:T(8,128)(2,1)}, u32[]{:S(2)}) copy-start(bf16[384,8,8]{0,2,1:T(8,128)(2,1)} %param.23) | copy-start | bytes 147460
  0.6 2.0 %copy-start.4 = (bf16[192,16,16]{0,2,1:T(8,128)(2,1)S(1)}, bf16[192,16,16]{0,2,1:T(8,128)(2,1)}, u32[]{:S(2)}) copy-start(bf16[192,16,16]{0,2,1:T(8,128)(2,1)} %param.22) | copy-start | bytes 294916
  0.7 2.0 %copy-start.1 = (bf16[96,32,32]{0,2,1:T(8,128)(2,1)S(1)}, bf16[96,32,32]{0,2,1:T(8,128)(2,1)}, u32[]{:S(2)}) copy-start(bf16[96,32,32]{0,2,1:T(8,128)(2,1)} %param.21) | copy-start | bytes 589828
  3.5 14.6 %copy-start = (bf16[1,576,864]{2,1,0:T(8,128)(2,1)S(1)}, bf16[1,576,864]{2,1,0:T(8,128)(2,1)}, u32[]{:S(2)}) copy-start(bf16[1,576,864]{2,1,0:T(8,128)(2,1)} %param.38) | copy-start | bytes 2985988
  3.5 14.6 %copy-start.10 = (bf16[2,48,432]{2,1,0:T(8,128)(2,1)S(1)}, bf16[2,48,432]{2,1,0:T(8,128)(2,1)}, u32[]{:S(2)}) copy-start(bf16[2,48,432]{2,1,0:T(8,128)(2,1)} %w0.1) | copy-start | bytes 248836
  3.5 14.6 %copy-start.15 = (f32[2,48]{1,0:T(2,128)S(1)}, f32[2,48]{1,0:T(2,128)}, u32[]{:S(2)}) copy-start(f32[2,48]{1,0:T(2,128)} %b0.1) | copy-start | bytes 1156
  3.5 14.6 %copy-start.16 = (f32[2,96]{1,0:T(2,128)S(1)}, f32[2,96]{1,0:T(2,128)}, u32[]{:S(2)}) copy-start(f32[2,96]{1,0:T(2,128)} %b1.1) | copy-start | bytes 2308
  3.5 8.1 %collective-permute-start = (bf16[592,128]{1,0:T(8,128)(2,1)}, bf16[592,128]{1,0:T(8,128)(2,1)S(1)}, u32[]{:S(2)}, u32[]{:S(2)}) collective-permute-start(bf16[592,128]{1,0:T(8,128)(2,1)} %get-tuple-element.22), channel_id=1, source_target_pairs={{0,8},{8,16},{16,24},{24,32},{32,40},{40,48},{48,56},{56,0},{1,9},... | collective-permute-start | bytes 454664 | tf_op jit(solution)/shard_map/ppermute | solution.py:483
  5.1 4.7 %collective-permute-start.1 = (bf16[240,128]{1,0:T(8,128)(2,1)}, bf16[240,128]{1,0:T(8,128)(2,1)S(1)}, u32[]{:S(2)}, u32[]{:S(2)}) collective-permute-start(bf16[240,128]{1,0:T(8,128)(2,1)} %get-tuple-element.23), channel_id=1, source_target_pairs={{0,56},{8,0},{16,8},{24,16},{32,24},{40,32},{48,40},{56,48},{1,57}... | collective-permute-start | bytes 184328 | tf_op jit(solution)/shard_map/ppermute | solution.py:483
  9.0 9.1 %copy-start.6 = (bf16[2,96,864]{2,1,0:T(8,128)(2,1)S(1)}, bf16[2,96,864]{2,1,0:T(8,128)(2,1)}, u32[]{:S(2)}) copy-start(bf16[2,96,864]{2,1,0:T(8,128)(2,1)} %w1.1) | copy-start | bytes 995332
  9.0 9.1 %copy-start.8 = (bf16[1,1,96,864]{3,2,1,0:T(8,128)(2,1)S(1)}, bf16[1,1,96,864]{3,2,1,0:T(8,128)(2,1)}, u32[]{:S(2)}) copy-start(bf16[1,1,96,864]{3,2,1,0:T(8,128)(2,1)} %param.36) | copy-start | bytes 497668
  9.1 9.1 %copy-start.9 = (bf16[1,3,48,432]{3,2,1,0:T(8,128)(2,1)S(1)}, bf16[1,3,48,432]{3,2,1,0:T(8,128)(2,1)}, u32[]{:S(2)}) copy-start(bf16[1,3,48,432]{3,2,1,0:T(8,128)(2,1)} %param.35) | copy-start | bytes 373252
  11.6 11.4 %copy-start.3 = (bf16[1,384,1728]{1,2,0:T(8,128)(2,1)S(1)}, bf16[1,384,1728]{1,2,0:T(8,128)(2,1)}, u32[]{:S(2)}) copy-start(bf16[1,384,1728]{1,2,0:T(8,128)(2,1)} %param.39) | copy-start | bytes 3981316
  12.0 10.9 %copy-start.2 = (bf16[2,192,1728]{2,1,0:T(8,128)(2,1)S(1)}, bf16[2,192,1728]{2,1,0:T(8,128)(2,1)}, u32[]{:S(2)}) copy-start(bf16[2,192,1728]{2,1,0:T(8,128)(2,1)} %rest_10_.1) | copy-start | bytes 3981316
  12.0 10.9 %copy-start.7 = (bf16[1,336,384]{2,1,0:T(8,128)(2,1)S(1)}, bf16[1,336,384]{2,1,0:T(8,128)(2,1)}, u32[]{:S(2)}) copy-start(bf16[1,336,384]{2,1,0:T(8,128)(2,1)} %param.34) | copy-start | bytes 774148
  12.0 10.9 %copy-start.11 = (bf16[1,144,192]{2,1,0:T(8,128)(2,1)S(1)}, bf16[1,144,192]{2,1,0:T(8,128)(2,1)}, u32[]{:S(2)}) copy-start(bf16[1,144,192]{2,1,0:T(8,128)(2,1)} %param.33) | copy-start | bytes 165892
  12.0 10.9 %copy-start.12 = (bf16[1,48,96]{2,1,0:T(8,128)(2,1)S(1)}, bf16[1,48,96]{2,1,0:T(8,128)(2,1)}, u32[]{:S(2)}) copy-start(bf16[1,48,96]{2,1,0:T(8,128)(2,1)} %param.32) | copy-start | bytes 27652
  12.0 10.9 %copy-start.13 = (f32[2,384]{1,0:T(2,128)S(1)}, f32[2,384]{1,0:T(2,128)}, u32[]{:S(2)}) copy-start(f32[2,384]{1,0:T(2,128)} %b3.1) | copy-start | bytes 9220
  12.1 10.9 %copy-start.14 = (f32[2,192]{1,0:T(2,128)S(1)}, f32[2,192]{1,0:T(2,128)}, u32[]{:S(2)}) copy-start(f32[2,192]{1,0:T(2,128)} %b2.1) | copy-start | bytes 4612
  12.1 10.8 %collective-permute-start.2 = (bf16[928,128]{1,0:T(8,128)(2,1)S(1)}, bf16[928,128]{1,0:T(8,128)(2,1)S(1)}, u32[]{:S(2)}, u32[]{:S(2)}) collective-permute-start(bf16[928,128]{1,0:T(8,128)(2,1)S(1)} %get-tuple-element.26), channel_id=1, source_target_pairs={{0,1},{1,2},{2,3},{3,4},{4,5},{5,6},{6,7},{7,0},{8,9},{9,10},{10,1... | collective-permute-start | bytes 712712 | tf_op jit(solution)/shard_map/ppermute | solution.py:483
  14.1 6.3 %collective-permute-start.3 = (bf16[400,128]{1,0:T(8,128)(2,1)S(1)}, bf16[400,128]{1,0:T(8,128)(2,1)S(1)}, u32[]{:S(2)}, u32[]{:S(2)}) collective-permute-start(bf16[400,128]{1,0:T(8,128)(2,1)S(1)} %get-tuple-element.27), channel_id=1, source_target_pairs={{0,7},{1,0},{2,1},{3,2},{4,3},{5,4},{6,5},{7,6},{8,15},{9,8},{10,9... | collective-permute-start | bytes 307208 | tf_op jit(solution)/shard_map/ppermute | solution.py:483
